TPU v7x, 32 devices: a whole 2x2x4 slice. The times are simulated.
32 devices in a mesh: rep: 8 (over z, x), tp: 4 (over y, core).
Axes of the slice: x: 2, y: 2, z: 4, core: 2. Of those that a mesh axis runs over, the one named last changes fastest.
Arguments:
- weight: bfloat16 [8, 2048, 7168], P('rep', None, 'tp'), may hold values from -6 to 6
- tokens: bfloat16 [8, 2, 512, 2048], P('rep'), may hold values from -6 to 6
- cotangent: bfloat16 [8, 2, 512, 7168], P('rep', None, None, 'tp'), may hold values from -6 to 6
- batch_order: int32 [8, 2], P('rep'), may hold values from 0 to 1, each once within a row
- step_index: int32 [1], replicated, may hold values from 0 to 999
Outputs:
- averaged: bfloat16 [8, 2048, 7168], P('rep', None, 'tp')
- losses: float32 [8, 2], P('rep')
Inputs may be any that keep to these rules, and one draw needn't show every extreme that they name: `batch_order`: each row lists 0 to 1 once.
All inputs are finite; a program needn't handle non-finite values.
Results may differ from a plain program's by a relative error of at most 0.009.
Values may be sent and summed in bfloat16 or wider, within the bound.
No kernel may reach another device: no remote copies, remote signals or barrier semaphores. Data moves between devices by JAX's collectives and lax.ppermute only.
A program may use at most 256 MiB of HBM per device.

v0:
```python
import jax
import jax.numpy as jnp
from jax import lax
from jax.sharding import PartitionSpec as P

FF = 7168


beta_first = 0.9
beta_second = 0.95
learn_rate = 0.05
decay_rate = 0.1
adam_eps = 1e-05
norm_eps = 1e-06


def shifted_2(array, axis, by):
    devices = lax.axis_size(axis)
    return lax.ppermute(array, axis, [(i, (i + by) % devices) for i in range(devices)])


def run_chain(weight, tokens, cotangent, order, combine_stats):
    width_scale = weight.shape[0] ** (-0.5)
    master = weight.astype(jnp.float32)
    moment = jnp.zeros(master.shape, jnp.float32)
    second = jnp.zeros(master.shape, jnp.float32)
    losses = []
    for local_step in range(tokens.shape[0]):
        chosen = order[local_step]
        inputs = lax.dynamic_index_in_dim(tokens, chosen, 0, keepdims=False)
        target = lax.dynamic_index_in_dim(cotangent, chosen, 0, keepdims=False).astype(jnp.float32)
        current = master.astype(jnp.bfloat16)
        hidden = jnp.dot(inputs, current, preferred_element_type=jnp.float32) * width_scale
        squares, inner = combine_stats(
            jnp.sum(hidden * hidden, axis=1), jnp.sum(target * hidden, axis=1)
        )
        radius = jnp.sqrt(squares / FF + norm_eps)
        losses.append(jnp.mean(inner / radius))
        token_count = inputs.shape[0]
        grad_rows = (
            target / radius[:, None] - hidden * (inner / (FF * radius**3))[:, None]
        ) / token_count
        grad_rows = grad_rows.astype(jnp.bfloat16)
        gradient = (
            lax.dot_general(
                inputs, grad_rows, (((0,), (0,)), ((), ())), preferred_element_type=jnp.float32
            )
            * width_scale
        )
        moment = beta_first * moment + (1.0 - beta_first) * gradient
        second = beta_second * second + (1.0 - beta_second) * gradient * gradient
        moment_hat = moment / (1.0 - beta_first ** (local_step + 1))
        second_hat = second / (1.0 - beta_second ** (local_step + 1))
        master = master - learn_rate * (
            moment_hat / (jnp.sqrt(second_hat) + adam_eps) + decay_rate * master
        )
    return (master.astype(jnp.bfloat16), jnp.stack(losses))


def own_stats(squares, inner):
    return lax.psum((squares, inner), "tp")


def shards(weight, tokens, cotangent, batch_order, step_index):
    levels = lax.axis_size("rep").bit_length() - 1
    hop_level = step_index[0] % levels
    final_weight, losses = run_chain(weight[0], tokens[0], cotangent[0], batch_order[0], own_stats)

    def make_final(exponent):

        def shifted():
            return shifted_2(final_weight, "rep", 2**exponent)

        return shifted

    peer_weight = lax.switch(hop_level, [make_final(exponent) for exponent in range(levels)])
    averaged = ((final_weight.astype(jnp.float32) + peer_weight.astype(jnp.float32)) * 0.5).astype(
        jnp.bfloat16
    )
    return (averaged[None], losses[None])


def solution(mesh):
    placed = (
        P("rep", None, "tp"),
        P("rep", None, None, None),
        P("rep", None, None, "tp"),
        P("rep", None),
        P(),
    )
    return jax.shard_map(
        shards,
        mesh=mesh,
        in_specs=placed,
        out_specs=(P("rep", None, "tp"), P("rep", None)),
        check_vma=False,
    )
```

profile of v0, /device:TPU:0, one launch (start us, length us, event | category | flops | bytes accessed | tf_op | source)
XLA Modules:
  0.0 272.3 jit_solution(16414603253847304148)
XLA Ops:
  1.3 1.3 fusion.55
  6.5 10.1 %multiply_reduce_fusion.1 = (f32[512]{0:T(512)S(1)}, f32[512]{0:T(512)S(1)}, f32[512,1792]{1,0:T(8,128)}) fusion(bf16[1,2,512,1792]{3,2,1,0:T(8,128)(2,1)} %param.10, s32[]{:T(128)S(6)} %select_n.17, bf16[1,2048,1792]{2,1,0:T(8,128)(2,1)} %param.8, bf16[1,2,512,2048]{3,2,1,0:T(8,128)(2,1)} %param.9), kind=kOutput, calls=%fused_computation.25 | convolution fusion | flops 3763600384 | bytes 14947328 | tf_op jit(solution)/shard_map/dot_general | solution.py:33
  16.6 8.6 %all-reduce.1 = (f32[512]{0:T(512)S(1)}, f32[512]{0:T(512)S(1)}) all-reduce(f32[512]{0:T(512)S(1)} %get-tuple-element.18, f32[512]{0:T(512)S(1)} %get-tuple-element.17), channel_id=1, replica_groups=mesh['rep'=8,'tp'=4] {'tp'}, use_global_device_ids=true, to_apply=%region_3.4 | all-reduce | flops 1024 | bytes 8192 | tf_op jit(solution)/shard_map/psum | solution.py:61
  25.2 0.6 divide_reduce_fusion.1
  26.4 0.0 copy-start.1
  26.4 0.0 copy-start.2
  26.4 0.0 copy-start.3
  26.5 12.9 %fusion.17 = f32[2048,1792]{1,0:T(8,128)} fusion(bf16[1,2,512,2048]{3,2,1,0:T(8,128)(2,1)} %param.9, s32[]{:T(128)S(6)} %select_n.17, f32[512,1792]{1,0:T(8,128)} %get-tuple-element.31, f32[512]{0:T(512)S(1)} %get-tuple-element.24, f32[512]{0:T(512)S(1)} %get-tuple-element.27, bf16[1,2,512,1792]{3,2,1,0:T(8,128)(2,1)} %param.10), kind=kOutput, calls=%fused_computation.28 | convolution fusion | flops 3763601408 | bytes 22287360 | tf_op jit(solution)/shard_map/dot_general | solution.py:45
  39.3 0.0 copy-done.1
  39.3 0.0 copy-done.2
  39.3 0.0 copy-done.3
  39.3 18.9 %multiply_reduce_fusion = (f32[512]{0:T(512)S(1)}, f32[512]{0:T(512)S(1)}, f32[512,1792]{1,0:T(8,128)}) fusion(bf16[1,2,512,1792]{3,2,1,0:T(8,128)(2,1)S(1)} %copy-done.3, s32[]{:T(128)S(6)} %select_n.18, f32[2048,1792]{1,0:T(8,128)} %fusion.17, bf16[1,2048,1792]{2,1,0:T(8,128)(2,1)S(1)} %copy-done.1, bf16[1,2,512,2048]{3,2,1,0:T(8,128)(2,1)S(1)} %copy-done.2), kind=kOutput, calls=%fused_computation.24 | convolution fusion | flops 3811310592 | bytes 29627392 | tf_op jit(solution)/shard_map/dot_general | solution.py:33
  58.3 5.7 %all-reduce = (f32[512]{0:T(512)S(1)}, f32[512]{0:T(512)S(1)}) all-reduce(f32[512]{0:T(512)S(1)} %get-tuple-element.16, f32[512]{0:T(512)S(1)} %get-tuple-element.15), channel_id=1, replica_groups=mesh['rep'=8,'tp'=4] {'tp'}, use_global_device_ids=true, to_apply=%region_7.8 | all-reduce | flops 1024 | bytes 8192 | tf_op jit(solution)/shard_map/psum | solution.py:61
  64.0 0.6 divide_reduce_fusion
  65.3 0.6 maximum_bitcast_fusion
  65.8 31.4 %subtract_convert_fusion = bf16[2048,1792]{1,0:T(8,128)(2,1)S(1)} fusion(f32[2048,1792]{1,0:T(8,128)} %fusion.17, bf16[1,2,512,2048]{3,2,1,0:T(8,128)(2,1)} %param.9, s32[]{:T(128)S(6)} %select_n.18, f32[512,1792]{1,0:T(8,128)} %get-tuple-element.32, f32[512]{0:T(512)S(1)} %get-tuple-element.26, f32[512]{0:T(512)S(1)} %get-tuple-element.28, ...), kind=kOutput, calls=%fused_computation.5 | convolution fusion | flops 3870031872 | bytes 36967424 | tf_op jit(solution)/shard_map/dot_general | solution.py:45
  97.2 0.0 copy-start
  97.2 3.0 %copy-done = bf16[2048,1792]{1,0:T(8,128)(2,1)} copy-done((bf16[2048,1792]{1,0:T(8,128)(2,1)}, bf16[2048,1792]{1,0:T(8,128)(2,1)S(1)}, u32[]{:S(2)}) %copy-start) | copy-done | bytes 7340056
  100.3 161.6 %conditional.4 = (bf16[2048,1792]{1,0:T(8,128)(2,1)}) conditional(s32[]{:T(128)} %clamp.3, bf16[2048,1792]{1,0:T(8,128)(2,1)S(1)} %subtract_convert_fusion, bf16[2048,1792]{1,0:T(8,128)(2,1)S(1)} %subtract_convert_fusion, bf16[2048,1792]{1,0:T(8,128)(2,1)S(1)} %subtract_convert_fusion), branch_computations={%region_8.9_spmd, %region_9.10_spmd, %region_10.11_spmd} | conditional | bytes 29360176
  100.3 1.7 collective-permute-start.1
  101.9 160.0 %collective-permute-done.1 = bf16[2048,1792]{1,0:T(8,128)(2,1)} collective-permute-done((bf16[2048,1792]{1,0:T(8,128)(2,1)S(1)}, bf16[2048,1792]{1,0:T(8,128)(2,1)}, u32[]{:S(2)}, u32[]{:S(2)}) %collective-permute-start.1) | collective-permute-done | bytes 7340064 | tf_op jit(solution)/shard_map/cond/branch_1_fun/ppermute | solution.py:19
  261.9 10.5 %fusion.2 = bf16[1,2048,1792]{2,1,0:T(8,128)(2,1)} fusion(bf16[2048,1792]{1,0:T(8,128)(2,1)} %get-tuple-element.33, bf16[2048,1792]{1,0:T(8,128)(2,1)} %copy-done), kind=kLoop, calls=%fused_computation.7 | loop fusion | flops 18350080 | bytes 22020096 | tf_op jit(solution)/shard_map/broadcast_in_dim | solution.py:80
Async XLA Ops:
  26.4 12.9 %copy-start.1 = (bf16[1,2048,1792]{2,1,0:T(8,128)(2,1)S(1)}, bf16[1,2048,1792]{2,1,0:T(8,128)(2,1)}, u32[]{:S(2)}) copy-start(bf16[1,2048,1792]{2,1,0:T(8,128)(2,1)} %param.8) | copy-start | bytes 22020100
  26.4 12.9 %copy-start.2 = (bf16[1,2,512,2048]{3,2,1,0:T(8,128)(2,1)S(1)}, bf16[1,2,512,2048]{3,2,1,0:T(8,128)(2,1)}, u32[]{:S(2)}) copy-start(bf16[1,2,512,2048]{3,2,1,0:T(8,128)(2,1)} %param.9) | copy-start | bytes 12582916
  26.4 12.9 %copy-start.3 = (bf16[1,2,512,1792]{3,2,1,0:T(8,128)(2,1)S(1)}, bf16[1,2,512,1792]{3,2,1,0:T(8,128)(2,1)}, u32[]{:S(2)}) copy-start(bf16[1,2,512,1792]{3,2,1,0:T(8,128)(2,1)} %param.10) | copy-start | bytes 11010052
  97.2 3.1 %copy-start = (bf16[2048,1792]{1,0:T(8,128)(2,1)}, bf16[2048,1792]{1,0:T(8,128)(2,1)S(1)}, u32[]{:S(2)}) copy-start(bf16[2048,1792]{1,0:T(8,128)(2,1)S(1)} %subtract_convert_fusion) | copy-start | bytes 22020100
  100.3 161.6 %collective-permute-start.1 = (bf16[2048,1792]{1,0:T(8,128)(2,1)S(1)}, bf16[2048,1792]{1,0:T(8,128)(2,1)}, u32[]{:S(2)}, u32[]{:S(2)}) collective-permute-start(bf16[2048,1792]{1,0:T(8,128)(2,1)S(1)} %param.1), channel_id=1, source_target_pairs={{0,8},{4,12},{8,16},{12,20},{16,24},{20,28},{24,0},{28,4},{1,9},{5... | collective-permute-start | bytes 22020104 | tf_op jit(solution)/shard_map/cond/branch_1_fun/ppermute | solution.py:19
where the time goes:
time: 273 us; the launch traced here: 272 us
  waiting for transfers between devices  160 us (59%)
  matrix products  73.3 us (27%)
  blocking collectives  14.3 us (5%)
  other arithmetic  12.3 us (5%)
  between operations  6.53 us (2%)
  local copies, waits for them, and re-layouts  4.38 us (2%)
    ppermute x1, waiting for transfers between devices, shifted_2(): lax.ppermute(array, axis, [(i, (i + by) % devices) for i in range(devices)])  160 us
    dot_general x2, matrix products, run_chain(): lax.dot_general(inputs, grad_rows, (((0,), (0,)), ((), ())), preferred_el...  44.2 us
    dot_general x2, matrix products, run_chain(): jnp.dot(inputs, current, preferred_element_type=jnp.float32) * width_scale  29 us
    psum x2, blocking collectives, own_stats(): return lax.psum((squares, inner), 'tp')  14.3 us
    broadcast_in_dim x2, other arithmetic, shards(): return (averaged[None], losses[None])  11 us
  transfers between devices with their start and end apart: 1, of which 1 were waited for; matrix products, arithmetic and copies ran while one was open for 0% of the time, Pallas kernels for 0%

commit v1 on v0

v1 whole, which is shorter than its diff:
```python
import functools

import jax
import jax.numpy as jnp
from jax import lax
from jax.experimental import pallas as pl
from jax.experimental.pallas import tpu as pltpu
from jax.sharding import PartitionSpec as P


beta_first = 0.9
beta_second = 0.95
learn_rate = 0.05
decay_rate = 0.1
adam_eps = 1e-05
norm_eps = 1e-06

F32 = jnp.float32
BF16 = jnp.bfloat16
KERNEL_VMEM = 16 * 1024 * 1024
ROWS = 512


def width_block(columns):
    for block in (256, 128):
        if columns % block == 0:
            return block
    return columns


def chunks_of(columns):
    block = width_block(columns)
    sizes = [block] * (columns // block)
    if block == 256 and len(sizes) > 1:
        sizes = [128] + sizes[1:] + [128]
    pieces = []
    low = 0
    for size in sizes:
        pieces.append((low, size))
        low += size
    return pieces


def lane_fold(values):
    total = values[:, :128]
    for at in range(128, values.shape[1], 128):
        total = total + values[:, at : at + 128]
    return total


def write_stats(stats_ref, squares, inner):
    stats_ref[0:1, :] = jnp.sum(squares[...].T, axis=0, keepdims=True)
    stats_ref[1:2, :] = jnp.sum(inner[...].T, axis=0, keepdims=True)


def token_factors(stats, units, tokens):
    squares, inner = stats[0:1, :], stats[1:2, :]
    radius = jnp.sqrt(squares / units + norm_eps)
    loss = jnp.sum(inner / radius, axis=1, keepdims=True) / tokens
    by_target = 1.0 / (radius * tokens)
    by_hidden = inner / (units * radius * radius * radius * tokens)
    pad = jnp.zeros((6, stats.shape[1]), F32)
    columns = jnp.concatenate([by_target, by_hidden, pad], axis=0).T
    return columns, loss


def forward_kernel(
    order, x_hbm, w_hbm, c_hbm,
    h_ref, xt_ref, stats_ref, x_ref, w_ref, c_ref, squares, inner, x_sem, w_sem, c_sem, *, scale, block,
):
    width, columns = w_ref.shape
    blocks = columns // block
    first, second = order[0], order[1]
    x_copies = [
        pltpu.make_async_copy(x_hbm.at[chosen], x_ref.at[at], x_sem.at[at])
        for at, chosen in enumerate((first, second))
    ]
    c_copies = [
        pltpu.make_async_copy(c_hbm.at[chosen], c_ref.at[at], c_sem.at[at])
        for at, chosen in enumerate((first, second))
    ]

    def w_copy(at):
        part = pl.ds(pl.multiple_of(at * block, block), block)
        return pltpu.make_async_copy(w_hbm.at[:, part], w_ref.at[:, part], w_sem.at[at])

    x_copies[0].start()
    w_copy(0).start()
    c_copies[0].start()
    for at in range(1, blocks):
        w_copy(at).start()
    x_copies[1].start()
    c_copies[1].start()
    squares[...] = jnp.zeros_like(squares)
    inner[...] = jnp.zeros_like(inner)
    piece = width // blocks // 128 * 128
    x_copies[0].wait()
    c_copies[0].wait()

    def one(at, carry):
        w_copy(at).wait()
        part = pl.ds(pl.multiple_of(at * block, block), block)
        hidden = jnp.dot(x_ref[0], w_ref[:, part], preferred_element_type=F32) * scale
        h_ref[:, part] = hidden
        target = c_ref[0, :, part].astype(F32)
        squares[...] += lane_fold(hidden * hidden)
        inner[...] += lane_fold(target * hidden)
        flip = pl.ds(pl.multiple_of(at * piece, 128), piece)
        xt_ref[flip, :] = x_ref[0, :, flip].T
        return carry

    lax.fori_loop(0, blocks, one, 0)
    if piece * blocks < width:
        xt_ref[piece * blocks :, :] = x_ref[0, :, piece * blocks :].T
    write_stats(stats_ref, squares, inner)
    x_copies[1].wait()
    c_copies[1].wait()


def forward(order, tokens, weight, target):
    steps, count, width = tokens.shape
    columns = weight.shape[1]
    block = width_block(columns)
    blocks = columns // block
    whole = pl.BlockSpec(memory_space=pltpu.VMEM)
    return pl.pallas_call(
        functools.partial(forward_kernel, scale=width**-0.5, block=block),
        out_shape=(
            pltpu.VMEM((count, columns), F32),
            pltpu.VMEM((width, count), BF16),
            jax.ShapeDtypeStruct((2, count), F32),
            pltpu.VMEM(tokens.shape, BF16),
            pltpu.VMEM(weight.shape, BF16),
            pltpu.VMEM(target.shape, BF16),
        ),
        in_specs=[pl.BlockSpec(memory_space=pltpu.SMEM)] + [pl.BlockSpec(memory_space=pl.ANY)] * 3,
        out_specs=(whole,) * 6,
        scratch_shapes=[
            pltpu.VMEM((count, 128), F32),
            pltpu.VMEM((count, 128), F32),
            pltpu.SemaphoreType.DMA((steps,)),
            pltpu.SemaphoreType.DMA((blocks,)),
            pltpu.SemaphoreType.DMA((steps,)),
        ],
        compiler_params=pltpu.CompilerParams(vmem_limit_bytes=KERNEL_VMEM),
        name="forward_first",
    )(order, tokens, weight, target)


def middle_kernel(
    parts, xt_ref, x_ref, w_ref, h_ref, c_ref,
    g_ref, h2_ref, xt2_ref, stats_ref, loss_ref, factors, squares, inner, *, scale, units, rows, block,
):
    count, columns = h_ref.shape
    width = w_ref.shape[0]
    blocks = columns // block
    factors[...], loss = token_factors(tree_sum([part[...] for part in parts]), units, count)
    loss_ref[...] = jnp.broadcast_to(loss, loss_ref.shape)
    squares[...] = jnp.zeros_like(squares)
    inner[...] = jnp.zeros_like(inner)
    piece = width // blocks // 128 * 128

    def one(at, carry):
        cols = pl.ds(pl.multiple_of(at * block, block), block)
        grad_rows = (
            c_ref[0, :, cols].astype(F32) * factors[:, 0:1] - h_ref[:, cols] * factors[:, 1:2]
        ).astype(BF16)
        total = None
        for low in range(0, width, rows):
            part = pl.ds(low, rows)
            gradient = jnp.dot(xt_ref[part, :], grad_rows, preferred_element_type=F32) * scale
            g_ref[part, cols] = gradient.astype(BF16)
            master = w_ref[part, cols].astype(F32)
            moved = gradient / (jnp.abs(gradient) + adam_eps)
            current = (master - learn_rate * (moved + decay_rate * master)).astype(BF16)
            term = jnp.dot(x_ref[1, :, part], current, preferred_element_type=F32)
            total = term if total is None else total + term
        hidden = total * scale
        h2_ref[:, cols] = hidden
        squares[...] += lane_fold(hidden * hidden)
        inner[...] += lane_fold(c_ref[1, :, cols].astype(F32) * hidden)
        flip = pl.ds(pl.multiple_of(at * piece, 128), piece)
        xt2_ref[flip, :] = x_ref[1, :, flip].T
        return carry

    lax.fori_loop(0, blocks, one, 0)
    if piece * blocks < width:
        xt2_ref[piece * blocks :, :] = x_ref[1, :, piece * blocks :].T
    write_stats(stats_ref, squares, inner)


def middle(stats, flipped, tokens, weight, hidden, target, units):
    _, count, width = tokens.shape
    columns = weight.shape[1]
    block = width_block(columns)
    whole = pl.BlockSpec(memory_space=pltpu.VMEM)
    return pl.pallas_call(
        functools.partial(
            middle_kernel, scale=width**-0.5, units=units, rows=min(ROWS, width), block=block
        ),
        out_shape=(
            pltpu.VMEM((width, columns), BF16),
            pltpu.VMEM((count, columns), F32),
            pltpu.VMEM((width, count), BF16),
            jax.ShapeDtypeStruct((2, count), F32),
            jax.ShapeDtypeStruct((1, 128), F32),
        ),
        in_specs=[[whole] * len(stats)] + [whole] * 5,
        out_specs=(whole,) * 5,
        scratch_shapes=[
            pltpu.VMEM((count, 8), F32),
            pltpu.VMEM((count, 128), F32),
            pltpu.VMEM((count, 128), F32),
        ],
        compiler_params=pltpu.CompilerParams(vmem_limit_bytes=KERNEL_VMEM),
        name="middle",
    )(stats, flipped, tokens, weight, hidden, target)


def last_kernel(
    parts, xt_ref, w_ref, g_ref, h_ref, c_ref, final_ref, loss_ref,
    *, scale, units, low, block, rows,
):
    count = h_ref.shape[0]
    cols = slice(low, low + block)
    columns, loss = token_factors(tree_sum([part[...] for part in parts]), units, count)
    loss_ref[...] = jnp.broadcast_to(loss, loss_ref.shape)
    grad_rows = (
        c_ref[1, :, cols].astype(F32) * columns[:, 0:1] - h_ref[:, cols] * columns[:, 1:2]
    ).astype(BF16)
    first_moment = beta_first * (1.0 - beta_first) / (1.0 - beta_first**2)
    fresh_moment = (1.0 - beta_first) / (1.0 - beta_first**2)
    first_second = beta_second * (1.0 - beta_second) / (1.0 - beta_second**2)
    fresh_second = (1.0 - beta_second) / (1.0 - beta_second**2)
    keep = 1.0 - learn_rate * decay_rate

    def one(at, carry):
        part = pl.ds(pl.multiple_of(at * rows, rows), rows)
        gradient = jnp.dot(xt_ref[part, :], grad_rows, preferred_element_type=F32) * scale
        first = g_ref[part, cols].astype(F32)
        master = w_ref[part, cols].astype(F32)
        master = keep * master - learn_rate * (first / (jnp.abs(first) + adam_eps))
        moment = first_moment * first + fresh_moment * gradient
        second = first_second * (first * first) + fresh_second * (gradient * gradient)
        master = keep * master - learn_rate * (moment / (jnp.sqrt(second) + adam_eps))
        final_ref[part, :] = master.astype(BF16)
        return carry

    lax.fori_loop(0, xt_ref.shape[0] // rows, one, 0)


def last(stats, flipped, weight, gradient, hidden, target, units, low, block):
    width, count = flipped.shape
    whole = pl.BlockSpec(memory_space=pltpu.VMEM)
    return pl.pallas_call(
        functools.partial(
            last_kernel, scale=width**-0.5, units=units, low=low, block=block, rows=min(256, width)
        ),
        out_shape=(
            pltpu.VMEM((width, block), BF16),
            jax.ShapeDtypeStruct((1, 128), F32),
        ),
        in_specs=[[whole] * len(stats)] + [whole] * 5,
        out_specs=(whole,) * 2,
        compiler_params=pltpu.CompilerParams(vmem_limit_bytes=KERNEL_VMEM),
        cost_estimate=pl.CostEstimate(
            flops=2 * width * count * block,
            bytes_accessed=2 * width * (3 * block + count) + 6 * count * block,
            transcendentals=3 * width * block,
        ),
        name="last",
    )(stats, flipped, weight, gradient, hidden, target)


def mean_kernel(own_ref, peer_ref, *refs, low, rows):
    out_ref, buffer, sems = refs[-3:]
    width, block = own_ref.shape
    copies = []
    for at in range(width // rows):
        part = slice(at * rows, (at + 1) * rows)
        buffer[part, :] = (
            (own_ref[part, :].astype(F32) + peer_ref[part, :].astype(F32)) * 0.5
        ).astype(BF16)
        copy = pltpu.make_async_copy(
            buffer.at[part, :], out_ref.at[part, low : low + block], sems.at[at]
        )
        copy.start()
        copies.append(copy)
    for copy in copies:
        copy.wait()


def mean_into(out, own, peer, columns, low):
    width, block = own.shape
    rows = min(512, width)
    whole = pl.BlockSpec(memory_space=pltpu.VMEM)
    anywhere = pl.BlockSpec(memory_space=pl.ANY)
    return pl.pallas_call(
        functools.partial(mean_kernel, low=low, rows=rows),
        out_shape=jax.ShapeDtypeStruct((width, columns), BF16),
        in_specs=[whole, whole] + ([] if out is None else [anywhere]),
        out_specs=anywhere,
        scratch_shapes=[
            pltpu.VMEM((width, block), BF16),
            pltpu.SemaphoreType.DMA((width // rows,)),
        ],
        input_output_aliases={} if out is None else {2: 0},
        compiler_params=pltpu.CompilerParams(vmem_limit_bytes=KERNEL_VMEM),
        cost_estimate=pl.CostEstimate(
            flops=2 * width * block, bytes_accessed=6 * width * block, transcendentals=0
        ),
        name="mean",
    )(*([own, peer] + ([] if out is None else [out])))


def tree_sum(parts):
    while len(parts) > 1:
        parts = [parts[at] + parts[at + 1] for at in range(0, len(parts), 2)]
    return parts[0]


def everyones(array, axis):
    devices = lax.axis_size(axis)
    if devices & (devices - 1):
        return [lax.psum(array, axis)]
    return [array] + [
        lax.ppermute(array, axis, [(i, i ^ flip) for i in range(devices)])
        for flip in range(1, devices)
    ]


def shifted(array, axis, by):
    devices = lax.axis_size(axis)
    return lax.ppermute(array, axis, [(i, (i + by) % devices) for i in range(devices)])


def shards(weight, tokens, cotangent, batch_order, step_index):
    weight, tokens, target, order = weight[0], tokens[0], cotangent[0], batch_order[0]
    _, columns = weight.shape
    units = columns * lax.axis_size("tp")
    levels = lax.axis_size("rep").bit_length() - 1
    hop_level = step_index[0] % levels

    pieces = chunks_of(columns)

    def chain(exponent):
        def run(order, tokens, weight, target):
            hidden, flipped, stats, tokens, weight, target = forward(order, tokens, weight, target)
            stats = everyones(stats, "tp")
            gradient, hidden, flipped, stats, loss_first = middle(
                stats, flipped, tokens, weight, hidden, target, units
            )
            stats = everyones(stats, "tp")
            finals, peers = [], []
            for at, (low, size) in enumerate(pieces):
                final, loss = last(
                    stats, flipped, weight, gradient, hidden, target, units, low, size
                )
                loss_second = loss if at == 0 else loss_second
                finals.append(final)
                peers.append(shifted(final, "rep", 2**exponent))
            out = None
            for (low, _), final, peer in zip(pieces, finals, peers):
                out = mean_into(out, final, peer, columns, low)
            return out, jnp.concatenate([loss_first[:, :1], loss_second[:, :1]], axis=1)

        return run

    averaged, losses = lax.switch(
        hop_level, [chain(exponent) for exponent in range(levels)], order, tokens, weight, target
    )
    return (averaged[None], losses)


def solution(mesh):
    placed = (
        P("rep", None, "tp"),
        P("rep", None, None, None),
        P("rep", None, None, "tp"),
        P("rep", None),
        P(),
    )
    return jax.shard_map(
        shards,
        mesh=mesh,
        in_specs=placed,
        out_specs=(P("rep", None, "tp"), P("rep", None)),
        check_vma=False,
    )
```

time: 273 us -> 205 us (0.75)
  matrix products: 73.3 us -> 0 us
  Pallas kernels: 0 us -> 63.2 us
  waiting for transfers between devices: 160 us -> 126 us
  blocking collectives: 14.3 us -> 0 us
  other arithmetic: 12.3 us -> 0.11 us
  starting transfers between devices: 1.66 us -> 13 us
  between operations: 6.53 us -> 1.31 us
  local copies, waits for them, and re-layouts: 4.38 us -> 0.51 us
    dot_general x4 -> x0, matrix products: 73.3 us -> none  [the longest x2 44.2 us: run_chain(): lax.dot_general(inputs, grad_rows, (((0,), (0,)), ((), ())), preferred_el...]
    pallas_call x0 -> x18, Pallas kernels: none -> 63.2 us  [the longest x8 28.5 us: last(): pl.pallas_call(functools.partial(last_kernel, scale=width ** (-0.5), unit...]
    ppermute x1 -> x14, waiting for transfers between devices: 160 us -> 126 us  [the longest x8 121 us: shifted(): lax.ppermute(array, axis, [(i, (i + by) % devices) for i in range(devices)])]
    psum x2 -> x0, blocking collectives: 14.3 us -> none  [own_stats(): return lax.psum((squares, inner), 'tp')]
    ppermute x1 -> x14, starting transfers between devices: 1.66 us -> 13 us  [the longest x8 7.93 us: shifted(): lax.ppermute(array, axis, [(i, (i + by) % devices) for i in range(devices)])]
    broadcast_in_dim x2 -> x0, other arithmetic: 11 us -> none  [shards(): return (averaged[None], losses[None])]
  transfers between devices with their start and end apart: 1 -> 14, of which waited for: 1 -> 9; matrix products, arithmetic and copies ran while one was open for 0% -> 0% of each run, Pallas kernels for 0% -> 16%
where the time goes in v1:
time: 205 us
  waiting for transfers between devices  126 us (61%)
  Pallas kernels  63.2 us (31%)
  starting transfers between devices  13 us (6%)
    ppermute x8, waiting for transfers between devices, shifted(): lax.ppermute(array, axis, [(i, (i + by) % devices) for i in range(devices)])  121 us
    pallas_call x8, Pallas kernels, last(): pl.pallas_call(functools.partial(last_kernel, scale=width ** (-0.5), unit...  28.5 us
    pallas_call x1, Pallas kernels, middle(): pl.pallas_call(functools.partial(middle_kernel, scale=width ** (-0.5), un...  16.2 us
    pallas_call x1, Pallas kernels, forward(): pl.pallas_call(functools.partial(forward_kernel, scale=width ** (-0.5), b...  10.3 us
    pallas_call x8, Pallas kernels, mean_into(): pl.pallas_call(functools.partial(mean_kernel, low=low, rows=rows), out_sh...  8.19 us
    ppermute x8, starting transfers between devices, shifted(): lax.ppermute(array, axis, [(i, (i + by) % devices) for i in range(devices)])  7.93 us
    ppermute x6, starting transfers between devices, everyones(): lax.ppermute(array, axis, [(i, i ^ flip) for i in range(devices)])  5.09 us
    ppermute x6, waiting for transfers between devices, everyones(): lax.ppermute(array, axis, [(i, i ^ flip) for i in range(devices)])  4.75 us
  transfers between devices with their start and end apart: 14, of which 9 were waited for; matrix products, arithmetic and copies ran while one was open for 0% of the time, Pallas kernels for 16%

profile of v1, /device:TPU:0, one launch (start us, length us, event | category | flops | bytes accessed | tf_op | source)
XLA Modules:
  0.0 204.8 jit_solution(1233864042640888009)
XLA Ops:
  1.3 203.0 %conditional.1 = (f32[1,2]{1,0:T(1,128)S(1)}, bf16[1,2048,1792]{2,1,0:T(8,128)(2,1)}) conditional(s32[]{:T(128)} %clamp.3, (s32[2]{0:T(128)}, bf16[2,512,2048]{2,1,0:T(8,128)(2,1)}, bf16[2048,1792]{1,0:T(8,128)(2,1)}, bf16[2,512,1792]{2,1,0:T(8,128)(2,1)}) %tuple.37, (s32[2]{0:T(128)}, bf16[2,512,2048]{2,1,0:T(8,128)(2,1)}, ...), branch_computations={%region_0.1_spmd, %region_1.2_spmd, %region_2.3_spmd} | conditional | flops 3765436416 | bytes 95781456 | solution.py:369
  1.5 10.3 %forward_first.4 = (f32[512,1792]{1,0:T(8,128)S(1)}, bf16[2048,512]{1,0:T(8,128)(2,1)S(1)}, f32[2,512]{1,0:T(2,128)S(1)}, bf16[2,512,2048]{2,1,0:T(8,128)(2,1)S(...) custom-call(s32[2]{0:T(128)} %get-tuple-element.49.order, ...), custom_call_target="tpu_custom_call" | custom-call | tf_op jit(solution)/shard_map/cond/branch_1_fun/forward_first/pallas_call | solution.py:126
  11.8 2.5 %collective-permute-start.16 = (f32[2,512]{1,0:T(2,128)S(1)}, f32[2,512]{1,0:T(2,128)S(1)}, u32[]{:S(2)}, u32[]{:S(2)}) collective-permute-start(f32[2,512]{1,0:T(2,128)S(1)} %get-tuple-element.53.parts_0_), channel_id=1, source_target_pairs={{0,3},{1,2},{2,1},{3,0},{4,7},{5,6},{6,5},{7,4},{8,11},{9,10},{10,... | collective-permute-start | bytes 12296 | tf_op jit(solution)/shard_map/cond/branch_1_fun/ppermute | solution.py:327
  15.6 2.3 %collective-permute-done.15.parts_2_ = f32[2,512]{1,0:T(2,128)S(1)} collective-permute-done((f32[2,512]{1,0:T(2,128)S(1)}, f32[2,512]{1,0:T(2,128)S(1)}, u32[]{:S(2)}, u32[]{:S(2)}) %collective-permute-start.15) | collective-permute-done | bytes 4128 | tf_op jit(solution)/shard_map/cond/branch_1_fun/ppermute | solution.py:327
  17.9 16.2 %middle.4 = (bf16[2048,1792]{1,0:T(8,128)(2,1)S(1)}, f32[512,1792]{1,0:T(8,128)S(1)}, bf16[2048,512]{1,0:T(8,128)(2,1)S(1)}, f32[2,512]{1,0:T(2,128)S(1)}, f32[1,128]{1,0:T(1,128)S(1)}) custom-call(f32[2,512]{1,0:T(2,128)S(1)} %get-tuple-element.53.parts_0_, f32[2,512]{1,0:T(2,128)S(1)} %collective-permute-done.14.parts_1_, ...), custom_call_target="tpu_custom_call" | custom-call | tf_op jit(solution)/shard_map/cond/branch_1_fun/middle/pallas_call | solution.py:197
  36.0 1.2 collective-permute-done.19.parts_3_
  37.9 3.8 %last.38 = (bf16[2048,256]{1,0:T(8,128)(2,1)S(1)}, f32[1,128]{1,0:T(1,128)}) custom-call(f32[2,512]{1,0:T(2,128)S(1)} %get-tuple-element.60.parts_0_, f32[2,512]{1,0:T(2,128)S(1)} %collective-permute-done.17.parts_1_, f32[2,512]{1,0:T(2,128)S(1)} %collective-permute-done.18.parts_2_, f32[2,512]{1,0:T(2,128)S(1)} %collective-permute-done.19.parts_3_, ...), custom_call_target="tpu_custom_call" | custom-call | flops 536870912 | bytes 6029312 | tf_op jit(solution)/shard_map/cond/branch_1_fun/last/pallas_call | solution.py:255
  41.7 1.6 collective-permute-start.25
  43.3 2.6 %last.32 = (bf16[2048,128]{1,0:T(8,128)(2,1)S(1)}, f32[1,128]{1,0:T(1,128)S(1)}) custom-call(f32[2,512]{1,0:T(2,128)S(1)} %get-tuple-element.60.parts_0_, f32[2,512]{1,0:T(2,128)S(1)} %collective-permute-done.17.parts_1_, f32[2,512]{1,0:T(2,128)S(1)} %collective-permute-done.18.parts_2_, f32[2,512]{1,0:T(2,128)S(1)} %collective-permute-done.19.parts_3_, ...), custom_call_target="tpu_custom_call" | custom-call | flops 268435456 | bytes 4063232 | tf_op jit(solution)/shard_map/cond/branch_1_fun/last/pallas_call | solution.py:255
  45.9 1.6 collective-permute-start.27
  47.5 3.8 %last.39 = (bf16[2048,256]{1,0:T(8,128)(2,1)S(1)}, f32[1,128]{1,0:T(1,128)}) custom-call(f32[2,512]{1,0:T(2,128)S(1)} %get-tuple-element.60.parts_0_, f32[2,512]{1,0:T(2,128)S(1)} %collective-permute-done.17.parts_1_, f32[2,512]{1,0:T(2,128)S(1)} %collective-permute-done.18.parts_2_, f32[2,512]{1,0:T(2,128)S(1)} %collective-permute-done.19.parts_3_, ...), custom_call_target="tpu_custom_call" | custom-call | flops 536870912 | bytes 6029312 | tf_op jit(solution)/shard_map/cond/branch_1_fun/last/pallas_call | solution.py:255
  51.3 1.6 collective-permute-start.26
  52.9 3.8 %last.35 = (bf16[2048,256]{1,0:T(8,128)(2,1)S(1)}, f32[1,128]{1,0:T(1,128)}) custom-call(f32[2,512]{1,0:T(2,128)S(1)} %get-tuple-element.60.parts_0_, f32[2,512]{1,0:T(2,128)S(1)} %collective-permute-done.17.parts_1_, f32[2,512]{1,0:T(2,128)S(1)} %collective-permute-done.18.parts_2_, f32[2,512]{1,0:T(2,128)S(1)} %collective-permute-done.19.parts_3_, ...), custom_call_target="tpu_custom_call" | custom-call | flops 536870912 | bytes 6029312 | tf_op jit(solution)/shard_map/cond/branch_1_fun/last/pallas_call | solution.py:255
  57.0 3.8 %last.36 = (bf16[2048,256]{1,0:T(8,128)(2,1)S(1)}, f32[1,128]{1,0:T(1,128)}) custom-call(f32[2,512]{1,0:T(2,128)S(1)} %get-tuple-element.60.parts_0_, f32[2,512]{1,0:T(2,128)S(1)} %collective-permute-done.17.parts_1_, f32[2,512]{1,0:T(2,128)S(1)} %collective-permute-done.18.parts_2_, f32[2,512]{1,0:T(2,128)S(1)} %collective-permute-done.19.parts_3_, ...), custom_call_target="tpu_custom_call" | custom-call | flops 536870912 | bytes 6029312 | tf_op jit(solution)/shard_map/cond/branch_1_fun/last/pallas_call | solution.py:255
  60.8 1.6 collective-permute-start.23
  62.4 3.8 %last.37 = (bf16[2048,256]{1,0:T(8,128)(2,1)S(1)}, f32[1,128]{1,0:T(1,128)}) custom-call(f32[2,512]{1,0:T(2,128)S(1)} %get-tuple-element.60.parts_0_, f32[2,512]{1,0:T(2,128)S(1)} %collective-permute-done.17.parts_1_, f32[2,512]{1,0:T(2,128)S(1)} %collective-permute-done.18.parts_2_, f32[2,512]{1,0:T(2,128)S(1)} %collective-permute-done.19.parts_3_, ...), custom_call_target="tpu_custom_call" | custom-call | flops 536870912 | bytes 6029312 | tf_op jit(solution)/shard_map/cond/branch_1_fun/last/pallas_call | solution.py:255
  66.2 14.6 %collective-permute-done.27.peer_ref = bf16[2048,128]{1,0:T(8,128)(2,1)S(1)} collective-permute-done((bf16[2048,128]{1,0:T(8,128)(2,1)S(1)}, bf16[2048,128]{1,0:T(8,128)(2,1)S(1)}, u32[]{:S(2)}, u32[]{:S(2)}) %collective-permute-start.27) | collective-permute-done | bytes 524320 | tf_op jit(solution)/shard_map/cond/branch_1_fun/ppermute | solution.py:334
  80.7 3.8 %last.34 = (bf16[2048,256]{1,0:T(8,128)(2,1)S(1)}, f32[1,128]{1,0:T(1,128)}) custom-call(f32[2,512]{1,0:T(2,128)S(1)} %get-tuple-element.60.parts_0_, f32[2,512]{1,0:T(2,128)S(1)} %collective-permute-done.17.parts_1_, f32[2,512]{1,0:T(2,128)S(1)} %collective-permute-done.18.parts_2_, f32[2,512]{1,0:T(2,128)S(1)} %collective-permute-done.19.parts_3_, ...), custom_call_target="tpu_custom_call" | custom-call | flops 536870912 | bytes 6029312 | tf_op jit(solution)/shard_map/cond/branch_1_fun/last/pallas_call | solution.py:255
  84.6 1.4 collective-permute-start.21
  85.9 2.9 %last.33 = (bf16[2048,128]{1,0:T(8,128)(2,1)S(1)}, f32[1,128]{1,0:T(1,128)}) custom-call(f32[2,512]{1,0:T(2,128)S(1)} %get-tuple-element.60.parts_0_, f32[2,512]{1,0:T(2,128)S(1)} %collective-permute-done.17.parts_1_, f32[2,512]{1,0:T(2,128)S(1)} %collective-permute-done.18.parts_2_, f32[2,512]{1,0:T(2,128)S(1)} %collective-permute-done.19.parts_3_, ...), custom_call_target="tpu_custom_call" | custom-call | flops 268435456 | bytes 4063232 | tf_op jit(solution)/shard_map/cond/branch_1_fun/last/pallas_call | solution.py:255
  88.8 14.4 %collective-permute-done.26.peer_ref = bf16[2048,256]{1,0:T(8,128)(2,1)S(1)} collective-permute-done((bf16[2048,256]{1,0:T(8,128)(2,1)S(1)}, bf16[2048,256]{1,0:T(8,128)(2,1)S(1)}, u32[]{:S(2)}, u32[]{:S(2)}) %collective-permute-start.26) | collective-permute-done | bytes 1048608 | tf_op jit(solution)/shard_map/cond/branch_1_fun/ppermute | solution.py:334
  106.4 64.2 %collective-permute-done.24.peer_ref = bf16[2048,256]{1,0:T(8,128)(2,1)S(1)} collective-permute-done((bf16[2048,256]{1,0:T(8,128)(2,1)S(1)}, bf16[2048,256]{1,0:T(8,128)(2,1)S(1)}, u32[]{:S(2)}, u32[]{:S(2)}) %collective-permute-start.24) | collective-permute-done | bytes 1048608 | tf_op jit(solution)/shard_map/cond/branch_1_fun/ppermute | solution.py:334
  173.9 19.2 %collective-permute-done.21.peer_ref = bf16[2048,256]{1,0:T(8,128)(2,1)S(1)} collective-permute-done((bf16[2048,256]{1,0:T(8,128)(2,1)S(1)}, bf16[2048,256]{1,0:T(8,128)(2,1)S(1)}, u32[]{:S(2)}, u32[]{:S(2)}) %collective-permute-start.21) | collective-permute-done | bytes 1048608 | tf_op jit(solution)/shard_map/cond/branch_1_fun/ppermute | solution.py:334
  194.2 8.8 %collective-permute-done.20.peer_ref = bf16[2048,128]{1,0:T(8,128)(2,1)S(1)} collective-permute-done((bf16[2048,128]{1,0:T(8,128)(2,1)S(1)}, bf16[2048,128]{1,0:T(8,128)(2,1)S(1)}, u32[]{:S(2)}, u32[]{:S(2)}) %collective-permute-start.20) | collective-permute-done | bytes 524320 | tf_op jit(solution)/shard_map/cond/branch_1_fun/ppermute | solution.py:334
  (26 shorter events, 12.9 us)
Async XLA Ops:
  11.8 3.8 %collective-permute-start.16 = (f32[2,512]{1,0:T(2,128)S(1)}, f32[2,512]{1,0:T(2,128)S(1)}, u32[]{:S(2)}, u32[]{:S(2)}) collective-permute-start(f32[2,512]{1,0:T(2,128)S(1)} %get-tuple-element.53.parts_0_), channel_id=1, source_target_pairs={{0,3},{1,2},{2,1},{3,0},{4,7},{5,6},{6,5},{7,4},{8,11},{9,10},{10,... | collective-permute-start | bytes 12296 | tf_op jit(solution)/shard_map/cond/branch_1_fun/ppermute | solution.py:327
  14.3 3.6 %collective-permute-start.15 = (f32[2,512]{1,0:T(2,128)S(1)}, f32[2,512]{1,0:T(2,128)S(1)}, u32[]{:S(2)}, u32[]{:S(2)}) collective-permute-start(f32[2,512]{1,0:T(2,128)S(1)} %get-tuple-element.53.parts_0_), channel_id=1, source_target_pairs={{0,2},{1,3},{2,0},{3,1},{4,6},{5,7},{6,4},{7,5},{8,10},{9,11},{10,... | collective-permute-start | bytes 12296 | tf_op jit(solution)/shard_map/cond/branch_1_fun/ppermute | solution.py:327
  14.9 3.0 %collective-permute-start.14 = (f32[2,512]{1,0:T(2,128)S(1)}, f32[2,512]{1,0:T(2,128)S(1)}, u32[]{:S(2)}, u32[]{:S(2)}) collective-permute-start(f32[2,512]{1,0:T(2,128)S(1)} %get-tuple-element.53.parts_0_), channel_id=1, source_target_pairs={{0,1},{1,0},{2,3},{3,2},{4,5},{5,4},{6,7},{7,6},{8,9},{9,8},{10,11... | collective-permute-start | bytes 12296 | tf_op jit(solution)/shard_map/cond/branch_1_fun/ppermute | solution.py:327
  34.1 3.1 %collective-permute-start.19 = (f32[2,512]{1,0:T(2,128)S(1)}, f32[2,512]{1,0:T(2,128)S(1)}, u32[]{:S(2)}, u32[]{:S(2)}) collective-permute-start(f32[2,512]{1,0:T(2,128)S(1)} %get-tuple-element.60.parts_0_), channel_id=1, source_target_pairs={{0,3},{1,2},{2,1},{3,0},{4,7},{5,6},{6,5},{7,4},{8,11},{9,10},{10,... | collective-permute-start | bytes 12296 | tf_op jit(solution)/shard_map/cond/branch_1_fun/ppermute | solution.py:327
  34.2 3.7 %collective-permute-start.18 = (f32[2,512]{1,0:T(2,128)S(1)}, f32[2,512]{1,0:T(2,128)S(1)}, u32[]{:S(2)}, u32[]{:S(2)}) collective-permute-start(f32[2,512]{1,0:T(2,128)S(1)} %get-tuple-element.60.parts_0_), channel_id=1, source_target_pairs={{0,2},{1,3},{2,0},{3,1},{4,6},{5,7},{6,4},{7,5},{8,10},{9,11},{10,... | collective-permute-start | bytes 12296 | tf_op jit(solution)/shard_map/cond/branch_1_fun/ppermute | solution.py:327
  35.3 2.5 %collective-permute-start.17 = (f32[2,512]{1,0:T(2,128)S(1)}, f32[2,512]{1,0:T(2,128)S(1)}, u32[]{:S(2)}, u32[]{:S(2)}) collective-permute-start(f32[2,512]{1,0:T(2,128)S(1)} %get-tuple-element.60.parts_0_), channel_id=1, source_target_pairs={{0,1},{1,0},{2,3},{3,2},{4,5},{5,4},{6,7},{7,6},{8,9},{9,8},{10,11... | collective-permute-start | bytes 12296 | tf_op jit(solution)/shard_map/cond/branch_1_fun/ppermute | solution.py:327
  41.7 42.9 %collective-permute-start.25 = (bf16[2048,256]{1,0:T(8,128)(2,1)S(1)}, bf16[2048,256]{1,0:T(8,128)(2,1)S(1)}, u32[]{:S(2)}, u32[]{:S(2)}) collective-permute-start(bf16[2048,256]{1,0:T(8,128)(2,1)S(1)} %get-tuple-element.70.own_ref), channel_id=1, source_target_pairs={{0,8},{4,12},{8,16},{12,20},{16,24},{20,28},{24,0},{28,4},{1,9},{5... | collective-permute-start | bytes 3145736 | tf_op jit(solution)/shard_map/cond/branch_1_fun/ppermute | solution.py:334
  45.9 34.9 %collective-permute-start.27 = (bf16[2048,128]{1,0:T(8,128)(2,1)S(1)}, bf16[2048,128]{1,0:T(8,128)(2,1)S(1)}, u32[]{:S(2)}, u32[]{:S(2)}) collective-permute-start(bf16[2048,128]{1,0:T(8,128)(2,1)S(1)} %get-tuple-element.72.own_ref), channel_id=1, source_target_pairs={{0,8},{4,12},{8,16},{12,20},{16,24},{20,28},{24,0},{28,4},{1,9},{5... | collective-permute-start | bytes 1572872 | tf_op jit(solution)/shard_map/cond/branch_1_fun/ppermute | solution.py:334
  51.3 51.9 %collective-permute-start.26 = (bf16[2048,256]{1,0:T(8,128)(2,1)S(1)}, bf16[2048,256]{1,0:T(8,128)(2,1)S(1)}, u32[]{:S(2)}, u32[]{:S(2)}) collective-permute-start(bf16[2048,256]{1,0:T(8,128)(2,1)S(1)} %get-tuple-element.71.own_ref), channel_id=1, source_target_pairs={{0,8},{4,12},{8,16},{12,20},{16,24},{20,28},{24,0},{28,4},{1,9},{5... | collective-permute-start | bytes 3145736 | tf_op jit(solution)/shard_map/cond/branch_1_fun/ppermute | solution.py:334
  56.7 116.1 %collective-permute-start.22 = (bf16[2048,256]{1,0:T(8,128)(2,1)S(1)}, bf16[2048,256]{1,0:T(8,128)(2,1)S(1)}, u32[]{:S(2)}, u32[]{:S(2)}) collective-permute-start(bf16[2048,256]{1,0:T(8,128)(2,1)S(1)} %get-tuple-element.67.own_ref), channel_id=1, source_target_pairs={{0,8},{4,12},{8,16},{12,20},{16,24},{20,28},{24,0},{28,4},{1,9},{5... | collective-permute-start | bytes 3145736 | tf_op jit(solution)/shard_map/cond/branch_1_fun/ppermute | solution.py:334
  60.8 110.9 %collective-permute-start.23 = (bf16[2048,256]{1,0:T(8,128)(2,1)S(1)}, bf16[2048,256]{1,0:T(8,128)(2,1)S(1)}, u32[]{:S(2)}, u32[]{:S(2)}) collective-permute-start(bf16[2048,256]{1,0:T(8,128)(2,1)S(1)} %get-tuple-element.68.own_ref), channel_id=1, source_target_pairs={{0,8},{4,12},{8,16},{12,20},{16,24},{20,28},{24,0},{28,4},{1,9},{5... | collective-permute-start | bytes 3145736 | tf_op jit(solution)/shard_map/cond/branch_1_fun/ppermute | solution.py:334
  80.7 89.9 %collective-permute-start.24 = (bf16[2048,256]{1,0:T(8,128)(2,1)S(1)}, bf16[2048,256]{1,0:T(8,128)(2,1)S(1)}, u32[]{:S(2)}, u32[]{:S(2)}) collective-permute-start(bf16[2048,256]{1,0:T(8,128)(2,1)S(1)} %get-tuple-element.69.own_ref), channel_id=1, source_target_pairs={{0,8},{4,12},{8,16},{12,20},{16,24},{20,28},{24,0},{28,4},{1,9},{5... | collective-permute-start | bytes 3145736 | tf_op jit(solution)/shard_map/cond/branch_1_fun/ppermute | solution.py:334
  84.6 108.5 %collective-permute-start.21 = (bf16[2048,256]{1,0:T(8,128)(2,1)S(1)}, bf16[2048,256]{1,0:T(8,128)(2,1)S(1)}, u32[]{:S(2)}, u32[]{:S(2)}) collective-permute-start(bf16[2048,256]{1,0:T(8,128)(2,1)S(1)} %get-tuple-element.66.own_ref), channel_id=1, source_target_pairs={{0,8},{4,12},{8,16},{12,20},{16,24},{20,28},{24,0},{28,4},{1,9},{5... | collective-permute-start | bytes 3145736 | tf_op jit(solution)/shard_map/cond/branch_1_fun/ppermute | solution.py:334
  103.2 99.7 %collective-permute-start.20 = (bf16[2048,128]{1,0:T(8,128)(2,1)S(1)}, bf16[2048,128]{1,0:T(8,128)(2,1)S(1)}, u32[]{:S(2)}, u32[]{:S(2)}) collective-permute-start(bf16[2048,128]{1,0:T(8,128)(2,1)S(1)} %get-tuple-element.65.own_ref), channel_id=1, source_target_pairs={{0,8},{4,12},{8,16},{12,20},{16,24},{20,28},{24,0},{28,4},{1,9},{5... | collective-permute-start | bytes 1572872 | tf_op jit(solution)/shard_map/cond/branch_1_fun/ppermute | solution.py:334
  204.3 0.5 copy-start

commit v2 on v1

--- a/solution.py
+++ b/solution.py
@@ -14,11 +14,18 @@
 decay_rate = 0.1
 adam_eps = 1e-05
 norm_eps = 1e-06
+tiny_square = 1e-30
 
 F32 = jnp.float32
 BF16 = jnp.bfloat16
 KERNEL_VMEM = 16 * 1024 * 1024
-ROWS = 512
+ROWS = 256
+LANES = 128
+TOKEN_ROWS = 64
+PIECE_CELLS = 256 * 256
+MEAN_CELLS = 128 * 256
+PIECE_COLUMNS = 512
+AHEAD = 3
 
 
 def width_block(columns):
@@ -29,10 +36,14 @@
 
 
 def chunks_of(columns):
-    block = width_block(columns)
-    sizes = [block] * (columns // block)
-    if block == 256 and len(sizes) > 1:
-        sizes = [128] + sizes[1:] + [128]
+    if columns % LANES or columns <= 2 * LANES:
+        return [(0, columns)]
+    sizes = [LANES]
+    left = columns - 2 * LANES
+    while left > 0:
+        sizes.append(min(PIECE_COLUMNS, left))
+        left -= sizes[-1]
+    sizes.append(LANES)
     pieces = []
     low = 0
     for size in sizes:
@@ -64,6 +75,10 @@
     return columns, loss
 
 
+def spread(column, lanes):
+    return jnp.broadcast_to(column, (column.shape[0], lanes))
+
+
 def forward_kernel(
     order, x_hbm, w_hbm, c_hbm,
     h_ref, xt_ref, stats_ref, x_ref, w_ref, c_ref, squares, inner, x_sem, w_sem, c_sem, *, scale, block,
@@ -71,34 +86,41 @@
     width, columns = w_ref.shape
     blocks = columns // block
     first, second = order[0], order[1]
-    x_copies = [
-        pltpu.make_async_copy(x_hbm.at[chosen], x_ref.at[at], x_sem.at[at])
-        for at, chosen in enumerate((first, second))
-    ]
-    c_copies = [
-        pltpu.make_async_copy(c_hbm.at[chosen], c_ref.at[at], c_sem.at[at])
-        for at, chosen in enumerate((first, second))
-    ]
+
+    def x_copy(at, chosen):
+        return pltpu.make_async_copy(x_hbm.at[chosen], x_ref.at[at], x_sem.at[at])
+
+    def c_copy(at):
+        part = pl.ds(pl.multiple_of(at * block, block), block)
+        return pltpu.make_async_copy(c_hbm.at[first, :, part], c_ref.at[0, :, part], c_sem.at[at])
 
     def w_copy(at):
         part = pl.ds(pl.multiple_of(at * block, block), block)
         return pltpu.make_async_copy(w_hbm.at[:, part], w_ref.at[:, part], w_sem.at[at])
 
-    x_copies[0].start()
-    w_copy(0).start()
-    c_copies[0].start()
-    for at in range(1, blocks):
+    later = pltpu.make_async_copy(c_hbm.at[second], c_ref.at[1], c_sem.at[blocks])
+    x_copy(0, first).start()
+    for at in range(min(AHEAD, blocks)):
         w_copy(at).start()
-    x_copies[1].start()
-    c_copies[1].start()
+        c_copy(at).start()
     squares[...] = jnp.zeros_like(squares)
     inner[...] = jnp.zeros_like(inner)
     piece = width // blocks // 128 * 128
-    x_copies[0].wait()
-    c_copies[0].wait()
+    x_copy(0, first).wait()
 
     def one(at, carry):
+        @pl.when(at + AHEAD < blocks)
+        def _():
+            w_copy(at + AHEAD).start()
+            c_copy(at + AHEAD).start()
+
+        @pl.when(at + AHEAD == blocks)
+        def _():
+            x_copy(1, second).start()
+            later.start()
+
         w_copy(at).wait()
+        c_copy(at).wait()
         part = pl.ds(pl.multiple_of(at * block, block), block)
         hidden = jnp.dot(x_ref[0], w_ref[:, part], preferred_element_type=F32) * scale
         h_ref[:, part] = hidden
@@ -110,11 +132,14 @@
         return carry
 
     lax.fori_loop(0, blocks, one, 0)
+    if blocks < AHEAD:
+        x_copy(1, second).start()
+        later.start()
     if piece * blocks < width:
         xt_ref[piece * blocks :, :] = x_ref[0, :, piece * blocks :].T
     write_stats(stats_ref, squares, inner)
-    x_copies[1].wait()
-    c_copies[1].wait()
+    x_copy(1, second).wait()
+    later.wait()
 
 
 def forward(order, tokens, weight, target):
@@ -140,7 +165,7 @@
             pltpu.VMEM((count, 128), F32),
             pltpu.SemaphoreType.DMA((steps,)),
             pltpu.SemaphoreType.DMA((blocks,)),
-            pltpu.SemaphoreType.DMA((steps,)),
+            pltpu.SemaphoreType.DMA((blocks + 1,)),
         ],
         compiler_params=pltpu.CompilerParams(vmem_limit_bytes=KERNEL_VMEM),
         name="forward_first",
@@ -149,41 +174,62 @@
 
 def middle_kernel(
     parts, xt_ref, x_ref, w_ref, h_ref, c_ref,
-    g_ref, h2_ref, xt2_ref, stats_ref, loss_ref, factors, squares, inner, *, scale, units, rows, block,
+    g_ref, h2_ref, xt2_ref, stats_ref, loss_ref,
+    by_target, by_hidden, even, odd, squares, inner, *, scale, units, rows, block,
 ):
     count, columns = h_ref.shape
     width = w_ref.shape[0]
     blocks = columns // block
-    factors[...], loss = token_factors(tree_sum([part[...] for part in parts]), units, count)
+    factors, loss = token_factors(tree_sum([part[...] for part in parts]), units, count)
+    by_target[...] = spread(factors[:, 0:1], block)
+    by_hidden[...] = spread(factors[:, 1:2], block)
     loss_ref[...] = jnp.broadcast_to(loss, loss_ref.shape)
     squares[...] = jnp.zeros_like(squares)
     inner[...] = jnp.zeros_like(inner)
     piece = width // blocks // 128 * 128
-
-    def one(at, carry):
-        cols = pl.ds(pl.multiple_of(at * block, block), block)
+    keep = 1.0 - learn_rate * decay_rate
+
+    def span(at):
+        return pl.ds(pl.multiple_of(at * block, block), block)
+
+    def update(at, current):
+        cols = span(at)
         grad_rows = (
-            c_ref[0, :, cols].astype(F32) * factors[:, 0:1] - h_ref[:, cols] * factors[:, 1:2]
+            c_ref[0, :, cols].astype(F32) * by_target[...] - h_ref[:, cols] * by_hidden[...]
         ).astype(BF16)
-        total = None
         for low in range(0, width, rows):
             part = pl.ds(low, rows)
-            gradient = jnp.dot(xt_ref[part, :], grad_rows, preferred_element_type=F32) * scale
-            g_ref[part, cols] = gradient.astype(BF16)
-            master = w_ref[part, cols].astype(F32)
-            moved = gradient / (jnp.abs(gradient) + adam_eps)
-            current = (master - learn_rate * (moved + decay_rate * master)).astype(BF16)
-            term = jnp.dot(x_ref[1, :, part], current, preferred_element_type=F32)
-            total = term if total is None else total + term
-        hidden = total * scale
+            product = jnp.dot(xt_ref[part, :], grad_rows, preferred_element_type=F32)
+            g_ref[part, cols] = product.astype(BF16)
+            moved = product / (jnp.abs(product) + adam_eps / scale)
+            current[part, :] = (
+                keep * w_ref[part, cols].astype(F32) - learn_rate * moved
+            ).astype(BF16)
+        flip = pl.ds(pl.multiple_of(at * piece, 128), piece)
+        xt2_ref[flip, :] = x_ref[1, :, flip].T
+
+    def project(at, current):
+        cols = span(at)
+        hidden = jnp.dot(x_ref[1], current[...], preferred_element_type=F32) * scale
         h2_ref[:, cols] = hidden
         squares[...] += lane_fold(hidden * hidden)
         inner[...] += lane_fold(c_ref[1, :, cols].astype(F32) * hidden)
-        flip = pl.ds(pl.multiple_of(at * piece, 128), piece)
-        xt2_ref[flip, :] = x_ref[1, :, flip].T
+
+    def pair(at, carry):
+        update(2 * at + 1, odd)
+        project(2 * at, even)
+        update(2 * at + 2, even)
+        project(2 * at + 1, odd)
         return carry
 
-    lax.fori_loop(0, blocks, one, 0)
+    update(0, even)
+    lax.fori_loop(0, (blocks - 1) // 2, pair, 0)
+    if blocks % 2:
+        project(blocks - 1, even)
+    else:
+        update(blocks - 1, odd)
+        project(blocks - 2, even)
+        project(blocks - 1, odd)
     if piece * blocks < width:
         xt2_ref[piece * blocks :, :] = x_ref[1, :, piece * blocks :].T
     write_stats(stats_ref, squares, inner)
@@ -208,7 +254,10 @@
         in_specs=[[whole] * len(stats)] + [whole] * 5,
         out_specs=(whole,) * 5,
         scratch_shapes=[
-            pltpu.VMEM((count, 8), F32),
+            pltpu.VMEM((count, block), F32),
+            pltpu.VMEM((count, block), F32),
+            pltpu.VMEM((width, block), BF16),
+            pltpu.VMEM((width, block), BF16),
             pltpu.VMEM((count, 128), F32),
             pltpu.VMEM((count, 128), F32),
         ],
@@ -217,92 +266,146 @@
     )(stats, flipped, tokens, weight, hidden, target)
 
 
-def last_kernel(
-    parts, xt_ref, w_ref, g_ref, h_ref, c_ref, final_ref, loss_ref,
-    *, scale, units, low, block, rows,
+def factors_kernel(*refs, units):
+    parts, (by_target, by_hidden, loss_ref) = refs[:-3], refs[-3:]
+    count = by_target.shape[0]
+    factors, loss = token_factors(tree_sum([part[...] for part in parts]), units, count)
+    by_target[...] = spread(factors[:, 0:1], LANES)
+    by_hidden[...] = spread(factors[:, 1:2], LANES)
+    loss_ref[...] = jnp.broadcast_to(loss, loss_ref.shape)
+
+
+def last_part(
+    by_target, by_hidden, xt_ref, w_ref, g_ref, h_ref, c_ref, final_ref, grad_rows,
+    *, scale, low, block, rows,
 ):
     count = h_ref.shape[0]
     cols = slice(low, low + block)
-    columns, loss = token_factors(tree_sum([part[...] for part in parts]), units, count)
-    loss_ref[...] = jnp.broadcast_to(loss, loss_ref.shape)
-    grad_rows = (
-        c_ref[1, :, cols].astype(F32) * columns[:, 0:1] - h_ref[:, cols] * columns[:, 1:2]
-    ).astype(BF16)
-    first_moment = beta_first * (1.0 - beta_first) / (1.0 - beta_first**2)
-    fresh_moment = (1.0 - beta_first) / (1.0 - beta_first**2)
-    first_second = beta_second * (1.0 - beta_second) / (1.0 - beta_second**2)
-    fresh_second = (1.0 - beta_second) / (1.0 - beta_second**2)
+
+    def prepare(at, carry):
+        part = pl.ds(pl.multiple_of(at * TOKEN_ROWS, TOKEN_ROWS), TOKEN_ROWS)
+        for lane in range(0, block, LANES):
+            here = slice(low + lane, low + lane + LANES)
+            grad_rows[part, lane : lane + LANES] = (
+                c_ref[1, part, here].astype(F32) * by_target[part, :]
+                - h_ref[part, here] * by_hidden[part, :]
+            ).astype(BF16)
+        return carry
+
+    lax.fori_loop(0, count // TOKEN_ROWS, prepare, 0)
+    bias_first = 1.0 - beta_first**2
+    bias_second = 1.0 - beta_second**2
+    old_moment = learn_rate * scale * beta_first * (1.0 - beta_first) / bias_first
+    new_moment = learn_rate * scale * (1.0 - beta_first) / bias_first
+    old_second = scale * scale * beta_second * (1.0 - beta_second) / bias_second
+    new_second = scale * scale * (1.0 - beta_second) / bias_second
     keep = 1.0 - learn_rate * decay_rate
 
     def one(at, carry):
         part = pl.ds(pl.multiple_of(at * rows, rows), rows)
-        gradient = jnp.dot(xt_ref[part, :], grad_rows, preferred_element_type=F32) * scale
+        product = jnp.dot(xt_ref[part, :], grad_rows[...], preferred_element_type=F32)
         first = g_ref[part, cols].astype(F32)
-        master = w_ref[part, cols].astype(F32)
-        master = keep * master - learn_rate * (first / (jnp.abs(first) + adam_eps))
-        moment = first_moment * first + fresh_moment * gradient
-        second = first_second * (first * first) + fresh_second * (gradient * gradient)
-        master = keep * master - learn_rate * (moment / (jnp.sqrt(second) + adam_eps))
-        final_ref[part, :] = master.astype(BF16)
+        moved = first / (jnp.abs(first) + adam_eps / scale)
+        moment = old_moment * first + new_moment * product
+        second = old_second * (first * first) + new_second * (product * product)
+        second = jnp.maximum(second, tiny_square)
+        fresh = moment / (second * lax.rsqrt(second) + adam_eps)
+        master = keep * keep * w_ref[part, cols].astype(F32)
+        final_ref[part, :] = (master - (keep * learn_rate * moved + fresh)).astype(BF16)
         return carry
 
     lax.fori_loop(0, xt_ref.shape[0] // rows, one, 0)
 
 
-def last(stats, flipped, weight, gradient, hidden, target, units, low, block):
-    width, count = flipped.shape
+def first_piece_kernel(*refs, units, parts, **sizes):
+    stats, operands, outs, grad_rows = refs[:parts], refs[parts:-5], refs[-5:-1], refs[-1]
+    final_ref, by_target, by_hidden, loss_ref = outs
+    factors_kernel(*stats, by_target, by_hidden, loss_ref, units=units)
+    last_part(by_target, by_hidden, *operands, final_ref, grad_rows, **sizes)
+
+
+def piece_call(kernel, outs, operands, width, count, block):
     whole = pl.BlockSpec(memory_space=pltpu.VMEM)
     return pl.pallas_call(
-        functools.partial(
-            last_kernel, scale=width**-0.5, units=units, low=low, block=block, rows=min(256, width)
-        ),
-        out_shape=(
-            pltpu.VMEM((width, block), BF16),
-            jax.ShapeDtypeStruct((1, 128), F32),
-        ),
-        in_specs=[[whole] * len(stats)] + [whole] * 5,
-        out_specs=(whole,) * 2,
+        kernel,
+        out_shape=outs,
+        in_specs=[whole] * len(operands),
+        out_specs=jax.tree.map(lambda _: whole, outs),
+        scratch_shapes=[pltpu.VMEM((count, block), BF16)],
         compiler_params=pltpu.CompilerParams(vmem_limit_bytes=KERNEL_VMEM),
         cost_estimate=pl.CostEstimate(
             flops=2 * width * count * block,
             bytes_accessed=2 * width * (3 * block + count) + 6 * count * block,
             transcendentals=3 * width * block,
         ),
-        name="last",
-    )(stats, flipped, weight, gradient, hidden, target)
-
-
-def mean_kernel(own_ref, peer_ref, *refs, low, rows):
+    )(*operands)
+
+
+def first_piece(stats, operands, units, low, block):
+    width, count = operands[0].shape
+    rows = min(PIECE_CELLS // block, width)
+    kernel = functools.partial(
+        first_piece_kernel, units=units, parts=len(stats), scale=width**-0.5, low=low, block=block, rows=rows
+    )
+    outs = (
+        pltpu.VMEM((width, block), BF16),
+        pltpu.VMEM((count, LANES), F32),
+        pltpu.VMEM((count, LANES), F32),
+        jax.ShapeDtypeStruct((1, LANES), F32),
+    )
+    return piece_call(kernel, outs, (*stats, *operands), width, count, block)
+
+
+def next_piece(factors, operands, low, block):
+    width, count = operands[0].shape
+    rows = min(PIECE_CELLS // block, width)
+    kernel = functools.partial(last_part, scale=width**-0.5, low=low, block=block, rows=rows)
+    outs = pltpu.VMEM((width, block), BF16)
+    return piece_call(kernel, outs, (*factors, *operands), width, count, block)
+
+
+def mean_kernel(own_ref, peer_ref, *refs, low, parts):
     out_ref, buffer, sems = refs[-3:]
     width, block = own_ref.shape
-    copies = []
-    for at in range(width // rows):
-        part = slice(at * rows, (at + 1) * rows)
-        buffer[part, :] = (
-            (own_ref[part, :].astype(F32) + peer_ref[part, :].astype(F32)) * 0.5
-        ).astype(BF16)
-        copy = pltpu.make_async_copy(
+    rows = width // parts
+    step = min(MEAN_CELLS // block, rows)
+
+    def copy(at):
+        part = pl.ds(pl.multiple_of(at * rows, rows), rows)
+        return pltpu.make_async_copy(
             buffer.at[part, :], out_ref.at[part, low : low + block], sems.at[at]
         )
-        copy.start()
-        copies.append(copy)
-    for copy in copies:
-        copy.wait()
+
+    def one(at, carry):
+        def inner(sub, carry):
+            part = pl.ds(pl.multiple_of(at * rows + sub * step, step), step)
+            buffer[part, :] = (
+                (own_ref[part, :].astype(F32) + peer_ref[part, :].astype(F32)) * 0.5
+            ).astype(BF16)
+            return carry
+
+        lax.fori_loop(0, rows // step, inner, 0)
+        copy(at).start()
+        return carry
+
+    lax.fori_loop(0, parts, one, 0)
+    for at in range(parts):
+        copy(at).wait()
 
 
 def mean_into(out, own, peer, columns, low):
     width, block = own.shape
-    rows = min(512, width)
+    parts = 4 if width % 512 == 0 else 1
     whole = pl.BlockSpec(memory_space=pltpu.VMEM)
     anywhere = pl.BlockSpec(memory_space=pl.ANY)
     return pl.pallas_call(
-        functools.partial(mean_kernel, low=low, rows=rows),
+        functools.partial(mean_kernel, low=low, parts=parts),
         out_shape=jax.ShapeDtypeStruct((width, columns), BF16),
         in_specs=[whole, whole] + ([] if out is None else [anywhere]),
         out_specs=anywhere,
         scratch_shapes=[
             pltpu.VMEM((width, block), BF16),
-            pltpu.SemaphoreType.DMA((width // rows,)),
+            pltpu.SemaphoreType.DMA((parts,)),
         ],
         input_output_aliases={} if out is None else {2: 0},
         compiler_params=pltpu.CompilerParams(vmem_limit_bytes=KERNEL_VMEM),
@@ -352,11 +455,12 @@
             )
             stats = everyones(stats, "tp")
             finals, peers = [], []
+            operands = (flipped, weight, gradient, hidden, target)
             for at, (low, size) in enumerate(pieces):
-                final, loss = last(
-                    stats, flipped, weight, gradient, hidden, target, units, low, size
-                )
-                loss_second = loss if at == 0 else loss_second
+                if at == 0:
+                    final, *factors, loss_second = first_piece(stats, operands, units, low, size)
+                else:
+                    final = next_piece(factors, operands, low, size)
                 finals.append(final)
                 peers.append(shifted(final, "rep", 2**exponent))
             out = None

time: 205 us -> 209 us (1.020)
  waiting for transfers between devices: 126 us -> 145 us
  Pallas kernels: 63.2 us -> 49.3 us
    ppermute x8 -> x5, waiting for transfers between devices: 121 us -> 140 us  [shifted(): lax.ppermute(array, axis, [(i, (i + by) % devices) for i in range(devices)])]
    pallas_call x16 -> x10, Pallas kernels: 36.7 us -> 29.8 us  [the longest x5 23 us: piece_call(): pl.pallas_call(kernel, out_shape=outs, in_specs=[whole] * len(operands),...]
    pallas_call x1, Pallas kernels: 16.2 us -> 10.8 us  [middle(): pl.pallas_call(functools.partial(middle_kernel, scale=width ** (-0.5), un...]
    ppermute x8 -> x5, starting transfers between devices: 7.93 us -> 6.69 us  [shifted(): lax.ppermute(array, axis, [(i, (i + by) % devices) for i in range(devices)])]
  transfers between devices with their start and end apart: 14 -> 11, of which waited for: 9 -> 6; matrix products, arithmetic and copies ran while one was open for 0% -> 0% of each run, Pallas kernels for 16% -> 7%
where the time goes in v2:
time: 209 us
  waiting for transfers between devices  145 us (69%)
  Pallas kernels  49.3 us (24%)
  starting transfers between devices  11.8 us (6%)
    ppermute x5, waiting for transfers between devices, shifted(): lax.ppermute(array, axis, [(i, (i + by) % devices) for i in range(devices)])  140 us
    pallas_call x5, Pallas kernels, piece_call(): pl.pallas_call(kernel, out_shape=outs, in_specs=[whole] * len(operands),...  23 us
    pallas_call x1, Pallas kernels, middle(): pl.pallas_call(functools.partial(middle_kernel, scale=width ** (-0.5), un...  10.8 us
    pallas_call x1, Pallas kernels, forward(): pl.pallas_call(functools.partial(forward_kernel, scale=width ** (-0.5), b...  8.72 us
    pallas_call x5, Pallas kernels, mean_into(): pl.pallas_call(functools.partial(mean_kernel, low=low, parts=parts), out_...  6.82 us
    ppermute x5, starting transfers between devices, shifted(): lax.ppermute(array, axis, [(i, (i + by) % devices) for i in range(devices)])  6.69 us
    ppermute x6, starting transfers between devices, everyones(): lax.ppermute(array, axis, [(i, i ^ flip) for i in range(devices)])  5.09 us
    ppermute x6, waiting for transfers between devices, everyones(): lax.ppermute(array, axis, [(i, i ^ flip) for i in range(devices)])  4.76 us
  transfers between devices with their start and end apart: 11, of which 6 were waited for; matrix products, arithmetic and copies ran while one was open for 0% of the time, Pallas kernels for 7%

profile of v2, /device:TPU:0, one launch (start us, length us, event | category | flops | bytes accessed | tf_op | source)
XLA Modules:
  0.0 209.1 jit_solution(10481789907346752565)
XLA Ops:
  1.3 207.3 %conditional.1 = (f32[1,2]{1,0:T(1,128)S(1)}, bf16[1,2048,1792]{2,1,0:T(8,128)(2,1)}) conditional(s32[]{:T(128)} %clamp.3, (s32[2]{0:T(128)}, bf16[2,512,2048]{2,1,0:T(8,128)(2,1)}, bf16[2048,1792]{1,0:T(8,128)(2,1)}, bf16[2,512,1792]{2,1,0:T(8,128)(2,1)}) %tuple.37, (s32[2]{0:T(128)}, bf16[2,512,2048]{2,1,0:T(8,128)(2,1)}, ...), branch_computations={%region_0.1_spmd, %region_1.2_spmd, %region_2.3_spmd} | conditional | flops 3765436416 | bytes 89489880 | solution.py:473
  1.5 8.7 %forward_first.4 = (f32[512,1792]{1,0:T(8,128)S(1)}, bf16[2048,512]{1,0:T(8,128)(2,1)S(1)}, f32[2,512]{1,0:T(2,128)S(1)}, bf16[2,512,2048]{2,1,0:T(8,128)(2,1)S(...) custom-call(s32[2]{0:T(128)} %get-tuple-element.44.order, ...), custom_call_target="tpu_custom_call" | custom-call | tf_op jit(solution)/shard_map/cond/branch_1_fun/forward_first/pallas_call | solution.py:151
  10.2 2.5 %collective-permute-start.13 = (f32[2,512]{1,0:T(2,128)S(1)}, f32[2,512]{1,0:T(2,128)S(1)}, u32[]{:S(2)}, u32[]{:S(2)}) collective-permute-start(f32[2,512]{1,0:T(2,128)S(1)} %get-tuple-element.48.parts_0_), channel_id=1, source_target_pairs={{0,3},{1,2},{2,1},{3,0},{4,7},{5,6},{6,5},{7,4},{8,11},{9,10},{10,... | collective-permute-start | bytes 12296 | tf_op jit(solution)/shard_map/cond/branch_1_fun/ppermute | solution.py:430
  14.1 2.3 %collective-permute-done.12.parts_2_ = f32[2,512]{1,0:T(2,128)S(1)} collective-permute-done((f32[2,512]{1,0:T(2,128)S(1)}, f32[2,512]{1,0:T(2,128)S(1)}, u32[]{:S(2)}, u32[]{:S(2)}) %collective-permute-start.12) | collective-permute-done | bytes 4128 | tf_op jit(solution)/shard_map/cond/branch_1_fun/ppermute | solution.py:430
  16.3 10.8 %middle.4 = (bf16[2048,1792]{1,0:T(8,128)(2,1)S(1)}, f32[512,1792]{1,0:T(8,128)S(1)}, bf16[2048,512]{1,0:T(8,128)(2,1)S(1)}, f32[2,512]{1,0:T(2,128)S(1)}, f32[1,128]{1,0:T(1,128)S(1)}) custom-call(f32[2,512]{1,0:T(2,128)S(1)} %get-tuple-element.48.parts_0_, f32[2,512]{1,0:T(2,128)S(1)} %collective-permute-done.11.parts_1_, ...), custom_call_target="tpu_custom_call" | custom-call | tf_op jit(solution)/shard_map/cond/branch_1_fun/middle/pallas_call | solution.py:243
  27.3 1.1 collective-permute-start.15
  28.4 0.7 collective-permute-start.14
  29.1 1.2 collective-permute-done.16.refs_3_
  30.9 1.9 branch_1_fun.5
  32.9 6.5 %branch_1_fun.9.own_ref = bf16[2048,512]{1,0:T(8,128)(2,1)S(1)} custom-call(f32[512,128]{1,0:T(8,128)S(1)} %get-tuple-element.60.by_target, f32[512,128]{1,0:T(8,128)S(1)} %get-tuple-element.61.by_hidden, bf16[2048,512]{1,0:T(8,128)(2,1)S(1)} %get-tuple-element.56.refs_4_.xt_ref, bf16[2048,1792]{1,0:T(8,128)(2,1)S(1)} %get-tuple-element.51.w_ref.refs_5_, ...), custom_call_target="tpu_custom_call" | custom-call | flops 1073741824 | bytes 9961472 | tf_op jit(solution)/shard_map/cond/branch_1_fun/pallas_call | solution.py:329
  39.4 6.5 %branch_1_fun.8.own_ref = bf16[2048,512]{1,0:T(8,128)(2,1)S(1)} custom-call(f32[512,128]{1,0:T(8,128)S(1)} %get-tuple-element.60.by_target, f32[512,128]{1,0:T(8,128)S(1)} %get-tuple-element.61.by_hidden, bf16[2048,512]{1,0:T(8,128)(2,1)S(1)} %get-tuple-element.56.refs_4_.xt_ref, bf16[2048,1792]{1,0:T(8,128)(2,1)S(1)} %get-tuple-element.51.w_ref.refs_5_, ...), custom_call_target="tpu_custom_call" | custom-call | flops 1073741824 | bytes 9961472 | tf_op jit(solution)/shard_map/cond/branch_1_fun/pallas_call | solution.py:329
  45.9 1.6 collective-permute-start.19
  47.5 1.6 collective-permute-start.20
  49.1 6.5 %branch_1_fun.7.own_ref = bf16[2048,512]{1,0:T(8,128)(2,1)S(1)} custom-call(f32[512,128]{1,0:T(8,128)S(1)} %get-tuple-element.60.by_target, f32[512,128]{1,0:T(8,128)S(1)} %get-tuple-element.61.by_hidden, bf16[2048,512]{1,0:T(8,128)(2,1)S(1)} %get-tuple-element.56.refs_4_.xt_ref, bf16[2048,1792]{1,0:T(8,128)(2,1)S(1)} %get-tuple-element.51.w_ref.refs_5_, ...), custom_call_target="tpu_custom_call" | custom-call | flops 1073741824 | bytes 9961472 | tf_op jit(solution)/shard_map/cond/branch_1_fun/pallas_call | solution.py:329
  55.6 1.6 collective-permute-start.18
  57.4 1.6 branch_1_fun.6.own_ref
  59.0 1.6 collective-permute-start.17
  60.7 136.6 %collective-permute-done.21.peer_ref = bf16[2048,128]{1,0:T(8,128)(2,1)S(1)} collective-permute-done((bf16[2048,128]{1,0:T(8,128)(2,1)S(1)}, bf16[2048,128]{1,0:T(8,128)(2,1)S(1)}, u32[]{:S(2)}, u32[]{:S(2)}) %collective-permute-start.21) | collective-permute-done | bytes 524320 | tf_op jit(solution)/shard_map/cond/branch_1_fun/ppermute | solution.py:437
  197.3 0.9 mean.20.refs_0_
  198.3 1.7 mean.21.refs_0_
  199.9 1.7 mean.22.refs_0_
  201.6 1.7 mean.23.refs_0_
  203.3 3.9 %collective-permute-done.17.peer_ref = bf16[2048,128]{1,0:T(8,128)(2,1)S(1)} collective-permute-done((bf16[2048,128]{1,0:T(8,128)(2,1)S(1)}, bf16[2048,128]{1,0:T(8,128)(2,1)S(1)}, u32[]{:S(2)}, u32[]{:S(2)}) %collective-permute-start.17) | collective-permute-done | bytes 524320 | tf_op jit(solution)/shard_map/cond/branch_1_fun/ppermute | solution.py:437
  207.2 0.9 mean.24
  (14 shorter events, 2.9 us)
Async XLA Ops:
  10.2 3.8 %collective-permute-start.13 = (f32[2,512]{1,0:T(2,128)S(1)}, f32[2,512]{1,0:T(2,128)S(1)}, u32[]{:S(2)}, u32[]{:S(2)}) collective-permute-start(f32[2,512]{1,0:T(2,128)S(1)} %get-tuple-element.48.parts_0_), channel_id=1, source_target_pairs={{0,3},{1,2},{2,1},{3,0},{4,7},{5,6},{6,5},{7,4},{8,11},{9,10},{10,... | collective-permute-start | bytes 12296 | tf_op jit(solution)/shard_map/cond/branch_1_fun/ppermute | solution.py:430
  12.7 3.6 %collective-permute-start.12 = (f32[2,512]{1,0:T(2,128)S(1)}, f32[2,512]{1,0:T(2,128)S(1)}, u32[]{:S(2)}, u32[]{:S(2)}) collective-permute-start(f32[2,512]{1,0:T(2,128)S(1)} %get-tuple-element.48.parts_0_), channel_id=1, source_target_pairs={{0,2},{1,3},{2,0},{3,1},{4,6},{5,7},{6,4},{7,5},{8,10},{9,11},{10,... | collective-permute-start | bytes 12296 | tf_op jit(solution)/shard_map/cond/branch_1_fun/ppermute | solution.py:430
  13.4 3.0 %collective-permute-start.11 = (f32[2,512]{1,0:T(2,128)S(1)}, f32[2,512]{1,0:T(2,128)S(1)}, u32[]{:S(2)}, u32[]{:S(2)}) collective-permute-start(f32[2,512]{1,0:T(2,128)S(1)} %get-tuple-element.48.parts_0_), channel_id=1, source_target_pairs={{0,1},{1,0},{2,3},{3,2},{4,5},{5,4},{6,7},{7,6},{8,9},{9,8},{10,11... | collective-permute-start | bytes 12296 | tf_op jit(solution)/shard_map/cond/branch_1_fun/ppermute | solution.py:430
  27.2 3.1 %collective-permute-start.16 = (f32[2,512]{1,0:T(2,128)S(1)}, f32[2,512]{1,0:T(2,128)S(1)}, u32[]{:S(2)}, u32[]{:S(2)}) collective-permute-start(f32[2,512]{1,0:T(2,128)S(1)} %get-tuple-element.55.refs_0_), channel_id=1, source_target_pairs={{0,3},{1,2},{2,1},{3,0},{4,7},{5,6},{6,5},{7,4},{8,11},{9,10},{10,... | collective-permute-start | bytes 12296 | tf_op jit(solution)/shard_map/cond/branch_1_fun/ppermute | solution.py:430
  27.3 3.7 %collective-permute-start.15 = (f32[2,512]{1,0:T(2,128)S(1)}, f32[2,512]{1,0:T(2,128)S(1)}, u32[]{:S(2)}, u32[]{:S(2)}) collective-permute-start(f32[2,512]{1,0:T(2,128)S(1)} %get-tuple-element.55.refs_0_), channel_id=1, source_target_pairs={{0,2},{1,3},{2,0},{3,1},{4,6},{5,7},{6,4},{7,5},{8,10},{9,11},{10,... | collective-permute-start | bytes 12296 | tf_op jit(solution)/shard_map/cond/branch_1_fun/ppermute | solution.py:430
  28.4 2.5 %collective-permute-start.14 = (f32[2,512]{1,0:T(2,128)S(1)}, f32[2,512]{1,0:T(2,128)S(1)}, u32[]{:S(2)}, u32[]{:S(2)}) collective-permute-start(f32[2,512]{1,0:T(2,128)S(1)} %get-tuple-element.55.refs_0_), channel_id=1, source_target_pairs={{0,1},{1,0},{2,3},{3,2},{4,5},{5,4},{6,7},{7,6},{8,9},{9,8},{10,11... | collective-permute-start | bytes 12296 | tf_op jit(solution)/shard_map/cond/branch_1_fun/ppermute | solution.py:430
  45.9 154.1 %collective-permute-start.19 = (bf16[2048,512]{1,0:T(8,128)(2,1)S(1)}, bf16[2048,512]{1,0:T(8,128)(2,1)S(1)}, u32[]{:S(2)}, u32[]{:S(2)}) collective-permute-start(bf16[2048,512]{1,0:T(8,128)(2,1)S(1)} %branch_1_fun.8.own_ref), channel_id=1, source_target_pairs={{0,8},{4,12},{8,16},{12,20},{16,24},{20,28},{24,0},{28,4},{1,9},{5... | collective-permute-start | bytes 6291464 | tf_op jit(solution)/shard_map/cond/branch_1_fun/ppermute | solution.py:437
  47.5 150.8 %collective-permute-start.20 = (bf16[2048,512]{1,0:T(8,128)(2,1)S(1)}, bf16[2048,512]{1,0:T(8,128)(2,1)S(1)}, u32[]{:S(2)}, u32[]{:S(2)}) collective-permute-start(bf16[2048,512]{1,0:T(8,128)(2,1)S(1)} %branch_1_fun.9.own_ref), channel_id=1, source_target_pairs={{0,8},{4,12},{8,16},{12,20},{16,24},{20,28},{24,0},{28,4},{1,9},{5... | collective-permute-start | bytes 6291464 | tf_op jit(solution)/shard_map/cond/branch_1_fun/ppermute | solution.py:437
  55.6 146.1 %collective-permute-start.18 = (bf16[2048,512]{1,0:T(8,128)(2,1)S(1)}, bf16[2048,512]{1,0:T(8,128)(2,1)S(1)}, u32[]{:S(2)}, u32[]{:S(2)}) collective-permute-start(bf16[2048,512]{1,0:T(8,128)(2,1)S(1)} %branch_1_fun.7.own_ref), channel_id=1, source_target_pairs={{0,8},{4,12},{8,16},{12,20},{16,24},{20,28},{24,0},{28,4},{1,9},{5... | collective-permute-start | bytes 6291464 | tf_op jit(solution)/shard_map/cond/branch_1_fun/ppermute | solution.py:437
  57.2 140.1 %collective-permute-start.21 = (bf16[2048,128]{1,0:T(8,128)(2,1)S(1)}, bf16[2048,128]{1,0:T(8,128)(2,1)S(1)}, u32[]{:S(2)}, u32[]{:S(2)}) collective-permute-start(bf16[2048,128]{1,0:T(8,128)(2,1)S(1)} %get-tuple-element.62.own_ref), channel_id=1, source_target_pairs={{0,8},{4,12},{8,16},{12,20},{16,24},{20,28},{24,0},{28,4},{1,9},{5... | collective-permute-start | bytes 1572872 | tf_op jit(solution)/shard_map/cond/branch_1_fun/ppermute | solution.py:437
  59.0 148.2 %collective-permute-start.17 = (bf16[2048,128]{1,0:T(8,128)(2,1)S(1)}, bf16[2048,128]{1,0:T(8,128)(2,1)S(1)}, u32[]{:S(2)}, u32[]{:S(2)}) collective-permute-start(bf16[2048,128]{1,0:T(8,128)(2,1)S(1)} %branch_1_fun.6.own_ref), channel_id=1, source_target_pairs={{0,8},{4,12},{8,16},{12,20},{16,24},{20,28},{24,0},{28,4},{1,9},{5... | collective-permute-start | bytes 1572872 | tf_op jit(solution)/shard_map/cond/branch_1_fun/ppermute | solution.py:437
  208.6 0.5 copy-start

commit v3 on v2

--- a/solution.py
+++ b/solution.py
@@ -35,21 +35,17 @@
     return columns
 
 
-def chunks_of(columns):
-    if columns % LANES or columns <= 2 * LANES:
-        return [(0, columns)]
-    sizes = [LANES]
-    left = columns - 2 * LANES
-    while left > 0:
-        sizes.append(min(PIECE_COLUMNS, left))
-        left -= sizes[-1]
-    sizes.append(LANES)
-    pieces = []
-    low = 0
-    for size in sizes:
-        pieces.append((low, size))
-        low += size
-    return pieces
+def chunks_of(width, columns):
+    if columns % LANES or columns <= 2 * LANES or width % (4 * LANES):
+        return [(slice(0, width), slice(0, columns))]
+    halves = (slice(0, width // 2), slice(width // 2, width))
+    pieces = [(half, slice(0, LANES)) for half in halves]
+    low = LANES
+    while low < columns - LANES:
+        high = min(low + PIECE_COLUMNS, columns - LANES)
+        pieces.append((slice(0, width), slice(low, high)))
+        low = high
+    return pieces + [(half, slice(low, columns)) for half in halves]
 
 
 def lane_fold(values):
@@ -64,12 +60,12 @@
     stats_ref[1:2, :] = jnp.sum(inner[...].T, axis=0, keepdims=True)
 
 
-def token_factors(stats, units, tokens):
-    squares, inner = stats[0:1, :], stats[1:2, :]
+def token_factors(stats, units, tokens, scale):
+    squares, inner = stats[0:1, :] * (scale * scale), stats[1:2, :] * scale
     radius = jnp.sqrt(squares / units + norm_eps)
     loss = jnp.sum(inner / radius, axis=1, keepdims=True) / tokens
     by_target = 1.0 / (radius * tokens)
-    by_hidden = inner / (units * radius * radius * radius * tokens)
+    by_hidden = scale * inner / (units * radius * radius * radius * tokens)
     pad = jnp.zeros((6, stats.shape[1]), F32)
     columns = jnp.concatenate([by_target, by_hidden, pad], axis=0).T
     return columns, loss
@@ -79,12 +75,28 @@
     return jnp.broadcast_to(column, (column.shape[0], lanes))
 
 
+def in_hbm(array):
+    return pltpu.with_memory_space_constraint(array, pltpu.HBM)
+
+
 def forward_kernel(
-    order, x_hbm, w_hbm, c_hbm,
-    h_ref, xt_ref, stats_ref, x_ref, w_ref, c_ref, squares, inner, x_sem, w_sem, c_sem, *, scale, block,
+    order_hbm, x_hbm, w_hbm, c_hbm, h_ref, xt_ref, stats_ref, x_ref, w_ref, c_ref,
+    order, squares, inner, order_sem, x_sem, w_sem, c_sem, *, block,
 ):
     width, columns = w_ref.shape
     blocks = columns // block
+    order_copy = pltpu.make_async_copy(order_hbm, order, order_sem)
+    order_copy.start()
+
+    def w_copy(at):
+        part = pl.ds(pl.multiple_of(at * block, block), block)
+        return pltpu.make_async_copy(w_hbm.at[:, part], w_ref.at[:, part], w_sem.at[at])
+
+    w_copy(0).start()
+    squares[...] = jnp.zeros_like(squares)
+    inner[...] = jnp.zeros_like(inner)
+    piece = width // blocks // 128 * 128
+    order_copy.wait()
     first, second = order[0], order[1]
 
     def x_copy(at, chosen):
@@ -94,18 +106,12 @@
         part = pl.ds(pl.multiple_of(at * block, block), block)
         return pltpu.make_async_copy(c_hbm.at[first, :, part], c_ref.at[0, :, part], c_sem.at[at])
 
-    def w_copy(at):
-        part = pl.ds(pl.multiple_of(at * block, block), block)
-        return pltpu.make_async_copy(w_hbm.at[:, part], w_ref.at[:, part], w_sem.at[at])
-
     later = pltpu.make_async_copy(c_hbm.at[second], c_ref.at[1], c_sem.at[blocks])
     x_copy(0, first).start()
-    for at in range(min(AHEAD, blocks)):
+    c_copy(0).start()
+    for at in range(1, min(AHEAD, blocks)):
         w_copy(at).start()
         c_copy(at).start()
-    squares[...] = jnp.zeros_like(squares)
-    inner[...] = jnp.zeros_like(inner)
-    piece = width // blocks // 128 * 128
     x_copy(0, first).wait()
 
     def one(at, carry):
@@ -122,7 +128,7 @@
         w_copy(at).wait()
         c_copy(at).wait()
         part = pl.ds(pl.multiple_of(at * block, block), block)
-        hidden = jnp.dot(x_ref[0], w_ref[:, part], preferred_element_type=F32) * scale
+        hidden = jnp.dot(x_ref[0], w_ref[:, part], preferred_element_type=F32)
         h_ref[:, part] = hidden
         target = c_ref[0, :, part].astype(F32)
         squares[...] += lane_fold(hidden * hidden)
@@ -149,7 +155,7 @@
     blocks = columns // block
     whole = pl.BlockSpec(memory_space=pltpu.VMEM)
     return pl.pallas_call(
-        functools.partial(forward_kernel, scale=width**-0.5, block=block),
+        functools.partial(forward_kernel, block=block),
         out_shape=(
             pltpu.VMEM((count, columns), F32),
             pltpu.VMEM((width, count), BF16),
@@ -158,18 +164,20 @@
             pltpu.VMEM(weight.shape, BF16),
             pltpu.VMEM(target.shape, BF16),
         ),
-        in_specs=[pl.BlockSpec(memory_space=pltpu.SMEM)] + [pl.BlockSpec(memory_space=pl.ANY)] * 3,
+        in_specs=[pl.BlockSpec(memory_space=pl.ANY)] * 4,
         out_specs=(whole,) * 6,
         scratch_shapes=[
+            pltpu.SMEM(order.shape, order.dtype),
             pltpu.VMEM((count, 128), F32),
             pltpu.VMEM((count, 128), F32),
+            pltpu.SemaphoreType.DMA(()),
             pltpu.SemaphoreType.DMA((steps,)),
             pltpu.SemaphoreType.DMA((blocks,)),
             pltpu.SemaphoreType.DMA((blocks + 1,)),
         ],
         compiler_params=pltpu.CompilerParams(vmem_limit_bytes=KERNEL_VMEM),
         name="forward_first",
-    )(order, tokens, weight, target)
+    )(in_hbm(order), in_hbm(tokens), in_hbm(weight), in_hbm(target))
 
 
 def middle_kernel(
@@ -180,7 +188,7 @@
     count, columns = h_ref.shape
     width = w_ref.shape[0]
     blocks = columns // block
-    factors, loss = token_factors(tree_sum([part[...] for part in parts]), units, count)
+    factors, loss = token_factors(tree_sum([part[...] for part in parts]), units, count, scale)
     by_target[...] = spread(factors[:, 0:1], block)
     by_hidden[...] = spread(factors[:, 1:2], block)
     loss_ref[...] = jnp.broadcast_to(loss, loss_ref.shape)
@@ -210,7 +218,7 @@
 
     def project(at, current):
         cols = span(at)
-        hidden = jnp.dot(x_ref[1], current[...], preferred_element_type=F32) * scale
+        hidden = jnp.dot(x_ref[1], current[...], preferred_element_type=F32)
         h2_ref[:, cols] = hidden
         squares[...] += lane_fold(hidden * hidden)
         inner[...] += lane_fold(c_ref[1, :, cols].astype(F32) * hidden)
@@ -266,10 +274,10 @@
     )(stats, flipped, tokens, weight, hidden, target)
 
 
-def factors_kernel(*refs, units):
+def factors_kernel(*refs, units, scale):
     parts, (by_target, by_hidden, loss_ref) = refs[:-3], refs[-3:]
     count = by_target.shape[0]
-    factors, loss = token_factors(tree_sum([part[...] for part in parts]), units, count)
+    factors, loss = token_factors(tree_sum([part[...] for part in parts]), units, count, scale)
     by_target[...] = spread(factors[:, 0:1], LANES)
     by_hidden[...] = spread(factors[:, 1:2], LANES)
     loss_ref[...] = jnp.broadcast_to(loss, loss_ref.shape)
@@ -277,10 +285,10 @@
 
 def last_part(
     by_target, by_hidden, xt_ref, w_ref, g_ref, h_ref, c_ref, final_ref, grad_rows,
-    *, scale, low, block, rows,
+    *, scale, tall, cols, rows,
 ):
     count = h_ref.shape[0]
-    cols = slice(low, low + block)
+    low, block = cols.start, cols.stop - cols.start
 
     def prepare(at, carry):
         part = pl.ds(pl.multiple_of(at * TOKEN_ROWS, TOKEN_ROWS), TOKEN_ROWS)
@@ -302,7 +310,8 @@
     keep = 1.0 - learn_rate * decay_rate
 
     def one(at, carry):
-        part = pl.ds(pl.multiple_of(at * rows, rows), rows)
+        here = pl.ds(pl.multiple_of(at * rows, rows), rows)
+        part = pl.ds(pl.multiple_of(tall.start + at * rows, rows), rows)
         product = jnp.dot(xt_ref[part, :], grad_rows[...], preferred_element_type=F32)
         first = g_ref[part, cols].astype(F32)
         moved = first / (jnp.abs(first) + adam_eps / scale)
@@ -311,70 +320,87 @@
         second = jnp.maximum(second, tiny_square)
         fresh = moment / (second * lax.rsqrt(second) + adam_eps)
         master = keep * keep * w_ref[part, cols].astype(F32)
-        final_ref[part, :] = (master - (keep * learn_rate * moved + fresh)).astype(BF16)
+        final_ref[here, :] = (master - (keep * learn_rate * moved + fresh)).astype(BF16)
         return carry
 
-    lax.fori_loop(0, xt_ref.shape[0] // rows, one, 0)
-
-
-def first_piece_kernel(*refs, units, parts, **sizes):
+    lax.fori_loop(0, final_ref.shape[0] // rows, one, 0)
+
+
+def first_piece_kernel(*refs, units, parts, scale, **sizes):
     stats, operands, outs, grad_rows = refs[:parts], refs[parts:-5], refs[-5:-1], refs[-1]
     final_ref, by_target, by_hidden, loss_ref = outs
-    factors_kernel(*stats, by_target, by_hidden, loss_ref, units=units)
-    last_part(by_target, by_hidden, *operands, final_ref, grad_rows, **sizes)
-
-
-def piece_call(kernel, outs, operands, width, count, block):
+    factors_kernel(*stats, by_target, by_hidden, loss_ref, units=units, scale=scale)
+    last_part(by_target, by_hidden, *operands, final_ref, grad_rows, scale=scale, **sizes)
+
+
+def piece_call(kernel, outs, operands, tall, cols, count, units):
     whole = pl.BlockSpec(memory_space=pltpu.VMEM)
+    height, block = tall.stop - tall.start, cols.stop - cols.start
+    width = operands[-4].shape[0]
     return pl.pallas_call(
-        kernel,
-        out_shape=outs,
+        functools.partial(
+            kernel, scale=width**-0.5, tall=tall, cols=cols, rows=min(PIECE_CELLS // block, height), **units
+        ),
+        out_shape=(pltpu.VMEM((height, block), BF16), *outs),
         in_specs=[whole] * len(operands),
-        out_specs=jax.tree.map(lambda _: whole, outs),
+        out_specs=(whole,) * (1 + len(outs)),
         scratch_shapes=[pltpu.VMEM((count, block), BF16)],
         compiler_params=pltpu.CompilerParams(vmem_limit_bytes=KERNEL_VMEM),
         cost_estimate=pl.CostEstimate(
-            flops=2 * width * count * block,
-            bytes_accessed=2 * width * (3 * block + count) + 6 * count * block,
-            transcendentals=3 * width * block,
+            flops=2 * height * count * block,
+            bytes_accessed=2 * height * (3 * block + count) + 6 * count * block,
+            transcendentals=3 * height * block,
         ),
     )(*operands)
 
 
-def first_piece(stats, operands, units, low, block):
-    width, count = operands[0].shape
-    rows = min(PIECE_CELLS // block, width)
-    kernel = functools.partial(
-        first_piece_kernel, units=units, parts=len(stats), scale=width**-0.5, low=low, block=block, rows=rows
-    )
+def first_piece(stats, operands, units, tall, cols):
+    count = operands[0].shape[1]
     outs = (
-        pltpu.VMEM((width, block), BF16),
         pltpu.VMEM((count, LANES), F32),
         pltpu.VMEM((count, LANES), F32),
         jax.ShapeDtypeStruct((1, LANES), F32),
     )
-    return piece_call(kernel, outs, (*stats, *operands), width, count, block)
-
-
-def next_piece(factors, operands, low, block):
-    width, count = operands[0].shape
-    rows = min(PIECE_CELLS // block, width)
-    kernel = functools.partial(last_part, scale=width**-0.5, low=low, block=block, rows=rows)
-    outs = pltpu.VMEM((width, block), BF16)
-    return piece_call(kernel, outs, (*factors, *operands), width, count, block)
-
-
-def mean_kernel(own_ref, peer_ref, *refs, low, parts):
+    extra = {"units": units, "parts": len(stats)}
+    return piece_call(first_piece_kernel, outs, (*stats, *operands), tall, cols, count, extra)
+
+
+def next_piece(factors, operands, tall, cols):
+    count = operands[0].shape[1]
+    return piece_call(last_part, (), (*factors, *operands), tall, cols, count, {})[0]
+
+
+def losses_kernel(first_ref, second_ref, out_ref, buffer, sem):
+    buffer[:, 0:1] = first_ref[:, 0:1]
+    buffer[:, 1:2] = second_ref[:, 0:1]
+    copy = pltpu.make_async_copy(buffer, out_ref, sem)
+    copy.start()
+    copy.wait()
+
+
+def losses_out(first, second):
+    whole = pl.BlockSpec(memory_space=pltpu.VMEM)
+    return pl.pallas_call(
+        losses_kernel,
+        out_shape=pltpu.HBM((1, 2), F32),
+        in_specs=[whole, whole],
+        out_specs=pl.BlockSpec(memory_space=pl.ANY),
+        scratch_shapes=[pltpu.VMEM((1, 2), F32), pltpu.SemaphoreType.DMA(())],
+        compiler_params=pltpu.CompilerParams(vmem_limit_bytes=KERNEL_VMEM),
+        name="losses",
+    )(first, second)
+
+
+def mean_kernel(own_ref, peer_ref, *refs, tall, cols, parts):
     out_ref, buffer, sems = refs[-3:]
-    width, block = own_ref.shape
-    rows = width // parts
+    height, block = own_ref.shape
+    rows = height // parts
     step = min(MEAN_CELLS // block, rows)
 
     def copy(at):
         part = pl.ds(pl.multiple_of(at * rows, rows), rows)
-        return pltpu.make_async_copy(
-            buffer.at[part, :], out_ref.at[part, low : low + block], sems.at[at]
-        )
+        there = pl.ds(pl.multiple_of(tall.start + at * rows, rows), rows)
+        return pltpu.make_async_copy(buffer.at[part, :], out_ref.at[there, cols], sems.at[at])
 
     def one(at, carry):
         def inner(sub, carry):
@@ -393,24 +419,24 @@
         copy(at).wait()
 
 
-def mean_into(out, own, peer, columns, low):
-    width, block = own.shape
-    parts = 4 if width % 512 == 0 else 1
+def mean_into(out, own, peer, shape, tall, cols):
+    height, block = own.shape
+    parts = 4 if height % (4 * LANES) == 0 else 1
     whole = pl.BlockSpec(memory_space=pltpu.VMEM)
     anywhere = pl.BlockSpec(memory_space=pl.ANY)
     return pl.pallas_call(
-        functools.partial(mean_kernel, low=low, parts=parts),
-        out_shape=jax.ShapeDtypeStruct((width, columns), BF16),
+        functools.partial(mean_kernel, tall=tall, cols=cols, parts=parts),
+        out_shape=jax.ShapeDtypeStruct(shape, BF16),
         in_specs=[whole, whole] + ([] if out is None else [anywhere]),
         out_specs=anywhere,
         scratch_shapes=[
-            pltpu.VMEM((width, block), BF16),
+            pltpu.VMEM((height, block), BF16),
             pltpu.SemaphoreType.DMA((parts,)),
         ],
         input_output_aliases={} if out is None else {2: 0},
         compiler_params=pltpu.CompilerParams(vmem_limit_bytes=KERNEL_VMEM),
         cost_estimate=pl.CostEstimate(
-            flops=2 * width * block, bytes_accessed=6 * width * block, transcendentals=0
+            flops=2 * height * block, bytes_accessed=6 * height * block, transcendentals=0
         ),
         name="mean",
     )(*([own, peer] + ([] if out is None else [out])))
@@ -439,12 +465,12 @@
 
 def shards(weight, tokens, cotangent, batch_order, step_index):
     weight, tokens, target, order = weight[0], tokens[0], cotangent[0], batch_order[0]
-    _, columns = weight.shape
+    width, columns = weight.shape
     units = columns * lax.axis_size("tp")
     levels = lax.axis_size("rep").bit_length() - 1
     hop_level = step_index[0] % levels
 
-    pieces = chunks_of(columns)
+    pieces = chunks_of(width, columns)
 
     def chain(exponent):
         def run(order, tokens, weight, target):
@@ -456,17 +482,17 @@
             stats = everyones(stats, "tp")
             finals, peers = [], []
             operands = (flipped, weight, gradient, hidden, target)
-            for at, (low, size) in enumerate(pieces):
+            for at, piece in enumerate(pieces):
                 if at == 0:
-                    final, *factors, loss_second = first_piece(stats, operands, units, low, size)
+                    final, *factors, loss_second = first_piece(stats, operands, units, *piece)
                 else:
-                    final = next_piece(factors, operands, low, size)
+                    final = next_piece(factors, operands, *piece)
                 finals.append(final)
                 peers.append(shifted(final, "rep", 2**exponent))
             out = None
-            for (low, _), final, peer in zip(pieces, finals, peers):
-                out = mean_into(out, final, peer, columns, low)
-            return out, jnp.concatenate([loss_first[:, :1], loss_second[:, :1]], axis=1)
+            for piece, final, peer in zip(pieces, finals, peers):
+                out = mean_into(out, final, peer, weight.shape, *piece)
+            return out, losses_out(loss_first, loss_second)
 
         return run
 

time: 209 us -> 208 us (level)
  waiting for transfers between devices: 145 us -> 142 us
    ppermute x5 -> x7, waiting for transfers between devices: 140 us -> 138 us  [shifted(): lax.ppermute(array, axis, [(i, (i + by) % devices) for i in range(devices)])]
    pallas_call x11 -> x16, Pallas kernels: 38.5 us -> 40.3 us  [the longest x7 23.2 us: piece_call(): pl.pallas_call(functools.partial(kernel, scale=width ** (-0.5), tall=tall...]
    ppermute x5 -> x7, starting transfers between devices: 6.69 us -> 6.69 us  [shifted(): lax.ppermute(array, axis, [(i, (i + by) % devices) for i in range(devices)])]
  transfers between devices with their start and end apart: 11 -> 13, of which waited for: 6 -> 7; matrix products, arithmetic and copies ran while one was open for 0% -> 0% of each run, Pallas kernels for 7% -> 8%
where the time goes in v3:
time: 208 us
  waiting for transfers between devices  142 us (68%)
  Pallas kernels  51.1 us (25%)
  starting transfers between devices  11.8 us (6%)
    ppermute x7, waiting for transfers between devices, shifted(): lax.ppermute(array, axis, [(i, (i + by) % devices) for i in range(devices)])  138 us
    pallas_call x7, Pallas kernels, piece_call(): pl.pallas_call(functools.partial(kernel, scale=width ** (-0.5), tall=tall...  23.2 us
    pallas_call x1, Pallas kernels, middle(): pl.pallas_call(functools.partial(middle_kernel, scale=width ** (-0.5), un...  10.9 us
    pallas_call x1, Pallas kernels, forward(): pl.pallas_call(functools.partial(forward_kernel, block=block), out_shape=...  8.46 us
    pallas_call x7, Pallas kernels, mean_into(): pl.pallas_call(functools.partial(mean_kernel, tall=tall, cols=cols, parts...  8.07 us
    ppermute x7, starting transfers between devices, shifted(): lax.ppermute(array, axis, [(i, (i + by) % devices) for i in range(devices)])  6.69 us
    ppermute x6, starting transfers between devices, everyones(): lax.ppermute(array, axis, [(i, i ^ flip) for i in range(devices)])  5.09 us
    ppermute x6, waiting for transfers between devices, everyones(): lax.ppermute(array, axis, [(i, i ^ flip) for i in range(devices)])  4.76 us
  transfers between devices with their start and end apart: 13, of which 7 were waited for; matrix products, arithmetic and copies ran while one was open for 0% of the time, Pallas kernels for 8%

profile of v3, /device:TPU:0, one launch (start us, length us, event | category | flops | bytes accessed | tf_op | source)
XLA Modules:
  0.0 207.6 jit_solution(14030227644468585863)
XLA Ops:
  1.3 206.2 %conditional.1 = (f32[1,2]{1,0:T(1,128)}, bf16[1,2048,1792]{2,1,0:T(8,128)(2,1)}) conditional(s32[]{:T(128)} %clamp.3, (s32[2]{0:T(128)}, bf16[2,512,2048]{2,1,0:T(8,128)(2,1)}, bf16[2048,1792]{1,0:T(8,128)(2,1)}, bf16[2,512,1792]{2,1,0:T(8,128)(2,1)}) %tuple.37, (s32[2]{0:T(128)}, bf16[2,512,2048]{2,1,0:T(8,128)(2,1)}, ...), branch_computations={%region_0.1_spmd, %region_1.2_spmd, %region_2.3_spmd} | conditional | flops 3765436416 | bytes 90276376 | solution.py:499
  1.5 8.5 %forward_first.4 = (f32[512,1792]{1,0:T(8,128)S(1)}, bf16[2048,512]{1,0:T(8,128)(2,1)S(1)}, f32[2,512]{1,0:T(2,128)S(1)}, bf16[2,512,2048]{2,1,0:T(8,128)(2,1)S(...) custom-call(s32[2]{0:T(128)} %get-tuple-element.44.order_hbm, ...), custom_call_target="tpu_custom_call" | custom-call | tf_op jit(solution)/shard_map/cond/branch_1_fun/forward_first/pallas_call | solution.py:157
  10.0 2.5 %collective-permute-start.15 = (f32[2,512]{1,0:T(2,128)S(1)}, f32[2,512]{1,0:T(2,128)S(1)}, u32[]{:S(2)}, u32[]{:S(2)}) collective-permute-start(f32[2,512]{1,0:T(2,128)S(1)} %get-tuple-element.48.parts_0_), channel_id=1, source_target_pairs={{0,3},{1,2},{2,1},{3,0},{4,7},{5,6},{6,5},{7,4},{8,11},{9,10},{10,... | collective-permute-start | bytes 12296 | tf_op jit(solution)/shard_map/cond/branch_1_fun/ppermute | solution.py:456
  13.8 2.3 %collective-permute-done.14.parts_2_ = f32[2,512]{1,0:T(2,128)S(1)} collective-permute-done((f32[2,512]{1,0:T(2,128)S(1)}, f32[2,512]{1,0:T(2,128)S(1)}, u32[]{:S(2)}, u32[]{:S(2)}) %collective-permute-start.14) | collective-permute-done | bytes 4128 | tf_op jit(solution)/shard_map/cond/branch_1_fun/ppermute | solution.py:456
  16.1 10.9 %middle.4 = (bf16[2048,1792]{1,0:T(8,128)(2,1)S(1)}, f32[512,1792]{1,0:T(8,128)S(1)}, bf16[2048,512]{1,0:T(8,128)(2,1)S(1)}, f32[2,512]{1,0:T(2,128)S(1)}, f32[1,128]{1,0:T(1,128)S(1)}) custom-call(f32[2,512]{1,0:T(2,128)S(1)} %get-tuple-element.48.parts_0_, f32[2,512]{1,0:T(2,128)S(1)} %collective-permute-done.13.parts_1_, ...), custom_call_target="tpu_custom_call" | custom-call | tf_op jit(solution)/shard_map/cond/branch_1_fun/middle/pallas_call | solution.py:251
  27.0 1.1 collective-permute-start.17
  28.9 1.2 collective-permute-done.18.refs_3_
  30.7 1.2 branch_1_fun.7
  31.9 6.5 %branch_1_fun.12.own_ref = bf16[2048,512]{1,0:T(8,128)(2,1)S(1)} custom-call(f32[512,128]{1,0:T(8,128)S(1)} %get-tuple-element.60.by_target, f32[512,128]{1,0:T(8,128)S(1)} %get-tuple-element.61.by_hidden, bf16[2048,512]{1,0:T(8,128)(2,1)S(1)} %get-tuple-element.56.refs_4_.xt_ref, bf16[2048,1792]{1,0:T(8,128)(2,1)S(1)} %get-tuple-element.51.w_ref.refs_5_, ...), custom_call_target="tpu_custom_call" | custom-call | flops 1073741824 | bytes 9961472 | tf_op jit(solution)/shard_map/cond/branch_1_fun/pallas_call | solution.py:340
  38.4 6.5 %branch_1_fun.11.own_ref = bf16[2048,512]{1,0:T(8,128)(2,1)S(1)} custom-call(f32[512,128]{1,0:T(8,128)S(1)} %get-tuple-element.60.by_target, f32[512,128]{1,0:T(8,128)S(1)} %get-tuple-element.61.by_hidden, bf16[2048,512]{1,0:T(8,128)(2,1)S(1)} %get-tuple-element.56.refs_4_.xt_ref, bf16[2048,1792]{1,0:T(8,128)(2,1)S(1)} %get-tuple-element.51.w_ref.refs_5_, ...), custom_call_target="tpu_custom_call" | custom-call | flops 1073741824 | bytes 9961472 | tf_op jit(solution)/shard_map/cond/branch_1_fun/pallas_call | solution.py:340
  44.9 1.6 collective-permute-start.22
  46.5 1.6 collective-permute-start.23
  48.1 6.5 %branch_1_fun.10.own_ref = bf16[2048,512]{1,0:T(8,128)(2,1)S(1)} custom-call(f32[512,128]{1,0:T(8,128)S(1)} %get-tuple-element.60.by_target, f32[512,128]{1,0:T(8,128)S(1)} %get-tuple-element.61.by_hidden, bf16[2048,512]{1,0:T(8,128)(2,1)S(1)} %get-tuple-element.56.refs_4_.xt_ref, bf16[2048,1792]{1,0:T(8,128)(2,1)S(1)} %get-tuple-element.51.w_ref.refs_5_, ...), custom_call_target="tpu_custom_call" | custom-call | flops 1073741824 | bytes 9961472 | tf_op jit(solution)/shard_map/cond/branch_1_fun/pallas_call | solution.py:340
  54.6 1.6 collective-permute-start.21
  56.2 0.8 branch_1_fun.13.own_ref
  57.3 1.6 collective-permute-start.25
  58.9 0.8 branch_1_fun.9.own_ref
  59.7 0.8 branch_1_fun.8.own_ref
  60.6 130.1 %collective-permute-done.24.peer_ref = bf16[1024,128]{1,0:T(8,128)(2,1)S(1)} collective-permute-done((bf16[1024,128]{1,0:T(8,128)(2,1)S(1)}, bf16[1024,128]{1,0:T(8,128)(2,1)S(1)}, u32[]{:S(2)}, u32[]{:S(2)}) %collective-permute-start.24) | collective-permute-done | bytes 262176 | tf_op jit(solution)/shard_map/cond/branch_1_fun/ppermute | solution.py:463
  190.7 5.6 %collective-permute-done.25.peer_ref = bf16[1024,128]{1,0:T(8,128)(2,1)S(1)} collective-permute-done((bf16[1024,128]{1,0:T(8,128)(2,1)S(1)}, bf16[1024,128]{1,0:T(8,128)(2,1)S(1)}, u32[]{:S(2)}, u32[]{:S(2)}) %collective-permute-start.25) | collective-permute-done | bytes 262176 | tf_op jit(solution)/shard_map/cond/branch_1_fun/ppermute | solution.py:463
  198.5 1.7 mean.30.refs_0_
  200.2 1.7 mean.31.refs_0_
  201.9 1.7 mean.32.refs_0_
  204.3 1.9 collective-permute-done.19.peer_ref
  (20 shorter events, 6.7 us)
Async XLA Ops:
  10.0 3.8 %collective-permute-start.15 = (f32[2,512]{1,0:T(2,128)S(1)}, f32[2,512]{1,0:T(2,128)S(1)}, u32[]{:S(2)}, u32[]{:S(2)}) collective-permute-start(f32[2,512]{1,0:T(2,128)S(1)} %get-tuple-element.48.parts_0_), channel_id=1, source_target_pairs={{0,3},{1,2},{2,1},{3,0},{4,7},{5,6},{6,5},{7,4},{8,11},{9,10},{10,... | collective-permute-start | bytes 12296 | tf_op jit(solution)/shard_map/cond/branch_1_fun/ppermute | solution.py:456
  12.5 3.6 %collective-permute-start.14 = (f32[2,512]{1,0:T(2,128)S(1)}, f32[2,512]{1,0:T(2,128)S(1)}, u32[]{:S(2)}, u32[]{:S(2)}) collective-permute-start(f32[2,512]{1,0:T(2,128)S(1)} %get-tuple-element.48.parts_0_), channel_id=1, source_target_pairs={{0,2},{1,3},{2,0},{3,1},{4,6},{5,7},{6,4},{7,5},{8,10},{9,11},{10,... | collective-permute-start | bytes 12296 | tf_op jit(solution)/shard_map/cond/branch_1_fun/ppermute | solution.py:456
  13.1 3.0 %collective-permute-start.13 = (f32[2,512]{1,0:T(2,128)S(1)}, f32[2,512]{1,0:T(2,128)S(1)}, u32[]{:S(2)}, u32[]{:S(2)}) collective-permute-start(f32[2,512]{1,0:T(2,128)S(1)} %get-tuple-element.48.parts_0_), channel_id=1, source_target_pairs={{0,1},{1,0},{2,3},{3,2},{4,5},{5,4},{6,7},{7,6},{8,9},{9,8},{10,11... | collective-permute-start | bytes 12296 | tf_op jit(solution)/shard_map/cond/branch_1_fun/ppermute | solution.py:456
  26.9 3.1 %collective-permute-start.18 = (f32[2,512]{1,0:T(2,128)S(1)}, f32[2,512]{1,0:T(2,128)S(1)}, u32[]{:S(2)}, u32[]{:S(2)}) collective-permute-start(f32[2,512]{1,0:T(2,128)S(1)} %get-tuple-element.55.refs_0_), channel_id=1, source_target_pairs={{0,3},{1,2},{2,1},{3,0},{4,7},{5,6},{6,5},{7,4},{8,11},{9,10},{10,... | collective-permute-start | bytes 12296 | tf_op jit(solution)/shard_map/cond/branch_1_fun/ppermute | solution.py:456
  27.0 3.7 %collective-permute-start.17 = (f32[2,512]{1,0:T(2,128)S(1)}, f32[2,512]{1,0:T(2,128)S(1)}, u32[]{:S(2)}, u32[]{:S(2)}) collective-permute-start(f32[2,512]{1,0:T(2,128)S(1)} %get-tuple-element.55.refs_0_), channel_id=1, source_target_pairs={{0,2},{1,3},{2,0},{3,1},{4,6},{5,7},{6,4},{7,5},{8,10},{9,11},{10,... | collective-permute-start | bytes 12296 | tf_op jit(solution)/shard_map/cond/branch_1_fun/ppermute | solution.py:456
  28.1 2.5 %collective-permute-start.16 = (f32[2,512]{1,0:T(2,128)S(1)}, f32[2,512]{1,0:T(2,128)S(1)}, u32[]{:S(2)}, u32[]{:S(2)}) collective-permute-start(f32[2,512]{1,0:T(2,128)S(1)} %get-tuple-element.55.refs_0_), channel_id=1, source_target_pairs={{0,1},{1,0},{2,3},{3,2},{4,5},{5,4},{6,7},{7,6},{8,9},{9,8},{10,11... | collective-permute-start | bytes 12296 | tf_op jit(solution)/shard_map/cond/branch_1_fun/ppermute | solution.py:456
  44.9 155.3 %collective-permute-start.22 = (bf16[2048,512]{1,0:T(8,128)(2,1)S(1)}, bf16[2048,512]{1,0:T(8,128)(2,1)S(1)}, u32[]{:S(2)}, u32[]{:S(2)}) collective-permute-start(bf16[2048,512]{1,0:T(8,128)(2,1)S(1)} %branch_1_fun.11.own_ref), channel_id=1, source_target_pairs={{0,8},{4,12},{8,16},{12,20},{16,24},{20,28},{24,0},{28,4},{1,9},{5... | collective-permute-start | bytes 6291464 | tf_op jit(solution)/shard_map/cond/branch_1_fun/ppermute | solution.py:463
  46.5 152.0 %collective-permute-start.23 = (bf16[2048,512]{1,0:T(8,128)(2,1)S(1)}, bf16[2048,512]{1,0:T(8,128)(2,1)S(1)}, u32[]{:S(2)}, u32[]{:S(2)}) collective-permute-start(bf16[2048,512]{1,0:T(8,128)(2,1)S(1)} %branch_1_fun.12.own_ref), channel_id=1, source_target_pairs={{0,8},{4,12},{8,16},{12,20},{16,24},{20,28},{24,0},{28,4},{1,9},{5... | collective-permute-start | bytes 6291464 | tf_op jit(solution)/shard_map/cond/branch_1_fun/ppermute | solution.py:463
  54.6 147.3 %collective-permute-start.21 = (bf16[2048,512]{1,0:T(8,128)(2,1)S(1)}, bf16[2048,512]{1,0:T(8,128)(2,1)S(1)}, u32[]{:S(2)}, u32[]{:S(2)}) collective-permute-start(bf16[2048,512]{1,0:T(8,128)(2,1)S(1)} %branch_1_fun.10.own_ref), channel_id=1, source_target_pairs={{0,8},{4,12},{8,16},{12,20},{16,24},{20,28},{24,0},{28,4},{1,9},{5... | collective-permute-start | bytes 6291464 | tf_op jit(solution)/shard_map/cond/branch_1_fun/ppermute | solution.py:463
  57.0 133.7 %collective-permute-start.24 = (bf16[1024,128]{1,0:T(8,128)(2,1)S(1)}, bf16[1024,128]{1,0:T(8,128)(2,1)S(1)}, u32[]{:S(2)}, u32[]{:S(2)}) collective-permute-start(bf16[1024,128]{1,0:T(8,128)(2,1)S(1)} %branch_1_fun.13.own_ref), channel_id=1, source_target_pairs={{0,8},{4,12},{8,16},{12,20},{16,24},{20,28},{24,0},{28,4},{1,9},{5... | collective-permute-start | bytes 786440 | tf_op jit(solution)/shard_map/cond/branch_1_fun/ppermute | solution.py:463
  57.3 139.0 %collective-permute-start.25 = (bf16[1024,128]{1,0:T(8,128)(2,1)S(1)}, bf16[1024,128]{1,0:T(8,128)(2,1)S(1)}, u32[]{:S(2)}, u32[]{:S(2)}) collective-permute-start(bf16[1024,128]{1,0:T(8,128)(2,1)S(1)} %get-tuple-element.62.own_ref), channel_id=1, source_target_pairs={{0,8},{4,12},{8,16},{12,20},{16,24},{20,28},{24,0},{28,4},{1,9},{5... | collective-permute-start | bytes 786440 | tf_op jit(solution)/shard_map/cond/branch_1_fun/ppermute | solution.py:463
  190.7 12.8 %collective-permute-start.20 = (bf16[1024,128]{1,0:T(8,128)(2,1)S(1)}, bf16[1024,128]{1,0:T(8,128)(2,1)S(1)}, u32[]{:S(2)}, u32[]{:S(2)}) collective-permute-start(bf16[1024,128]{1,0:T(8,128)(2,1)S(1)} %branch_1_fun.9.own_ref), channel_id=1, source_target_pairs={{0,8},{4,12},{8,16},{12,20},{16,24},{20,28},{24,0},{28,4},{1,9},{5... | collective-permute-start | bytes 786440 | tf_op jit(solution)/shard_map/cond/branch_1_fun/ppermute | solution.py:463
  196.3 9.9 %collective-permute-start.19 = (bf16[1024,128]{1,0:T(8,128)(2,1)S(1)}, bf16[1024,128]{1,0:T(8,128)(2,1)S(1)}, u32[]{:S(2)}, u32[]{:S(2)}) collective-permute-start(bf16[1024,128]{1,0:T(8,128)(2,1)S(1)} %branch_1_fun.8.own_ref), channel_id=1, source_target_pairs={{0,8},{4,12},{8,16},{12,20},{16,24},{20,28},{24,0},{28,4},{1,9},{5... | collective-permute-start | bytes 786440 | tf_op jit(solution)/shard_map/cond/branch_1_fun/ppermute | solution.py:463

commit v4 on v3

--- a/solution.py
+++ b/solution.py
@@ -110,20 +110,20 @@
     x_copy(0, first).start()
     c_copy(0).start()
     for at in range(1, min(AHEAD, blocks)):
-        w_copy(at).start()
-        c_copy(at).start()
+        w_copy(at).start(priority=1)
+        c_copy(at).start(priority=1)
     x_copy(0, first).wait()
 
     def one(at, carry):
         @pl.when(at + AHEAD < blocks)
         def _():
-            w_copy(at + AHEAD).start()
-            c_copy(at + AHEAD).start()
+            w_copy(at + AHEAD).start(priority=1)
+            c_copy(at + AHEAD).start(priority=1)
 
         @pl.when(at + AHEAD == blocks)
         def _():
-            x_copy(1, second).start()
-            later.start()
+            x_copy(1, second).start(priority=1)
+            later.start(priority=1)
 
         w_copy(at).wait()
         c_copy(at).wait()
@@ -468,7 +468,7 @@
     width, columns = weight.shape
     units = columns * lax.axis_size("tp")
     levels = lax.axis_size("rep").bit_length() - 1
-    hop_level = step_index[0] % levels
+    hop_level = lax.rem(step_index[0], levels)
 
     pieces = chunks_of(width, columns)
 

time: 208 us -> 207 us (level)
  no operation moved by 1% of the time
where the time goes in v4:
time: 207 us
  waiting for transfers between devices  142 us (69%)
  Pallas kernels  50.4 us (24%)
  starting transfers between devices  11.8 us (6%)
    ppermute x7, waiting for transfers between devices, shifted(): lax.ppermute(array, axis, [(i, (i + by) % devices) for i in range(devices)])  138 us
    pallas_call x7, Pallas kernels, piece_call(): pl.pallas_call(functools.partial(kernel, scale=width ** (-0.5), tall=tall...  23 us
    pallas_call x1, Pallas kernels, middle(): pl.pallas_call(functools.partial(middle_kernel, scale=width ** (-0.5), un...  10.6 us
    pallas_call x1, Pallas kernels, forward(): pl.pallas_call(functools.partial(forward_kernel, block=block), out_shape=...  8.15 us
    pallas_call x7, Pallas kernels, mean_into(): pl.pallas_call(functools.partial(mean_kernel, tall=tall, cols=cols, parts...  8.07 us
    ppermute x7, starting transfers between devices, shifted(): lax.ppermute(array, axis, [(i, (i + by) % devices) for i in range(devices)])  6.7 us
    ppermute x6, starting transfers between devices, everyones(): lax.ppermute(array, axis, [(i, i ^ flip) for i in range(devices)])  5.1 us
    ppermute x6, waiting for transfers between devices, everyones(): lax.ppermute(array, axis, [(i, i ^ flip) for i in range(devices)])  4.76 us
  transfers between devices with their start and end apart: 13, of which 7 were waited for; matrix products, arithmetic and copies ran while one was open for 0% of the time, Pallas kernels for 8%

profile of v4, /device:TPU:0, one launch (start us, length us, event | category | flops | bytes accessed | tf_op | source)
XLA Modules:
  0.0 207.0 jit_solution(7200330677516936549)
XLA Ops:
  1.3 205.5 %conditional.1 = (f32[1,2]{1,0:T(1,128)}, bf16[1,2048,1792]{2,1,0:T(8,128)(2,1)}) conditional(s32[]{:T(128)} %bitcast.3, (s32[2]{0:T(128)}, bf16[2,512,2048]{2,1,0:T(8,128)(2,1)}, bf16[2048,1792]{1,0:T(8,128)(2,1)}, bf16[2,512,1792]{2,1,0:T(8,128)(2,1)}) %tuple.37, (s32[2]{0:T(128)}, bf16[2,512,2048]{2,1,0:T(8,128)(2,1)}, ...), branch_computations={%region_0.0_spmd, %region_1.0_spmd, %region_2.0_spmd} | conditional | flops 3765436416 | bytes 90276376 | solution.py:499
  1.5 8.1 %forward_first.4 = (f32[512,1792]{1,0:T(8,128)S(1)}, bf16[2048,512]{1,0:T(8,128)(2,1)S(1)}, f32[2,512]{1,0:T(2,128)S(1)}, bf16[2,512,2048]{2,1,0:T(8,128)(2,1)S(...) custom-call(s32[2]{0:T(128)} %get-tuple-element.44.order_hbm, ...), custom_call_target="tpu_custom_call" | custom-call | tf_op jit(solution)/shard_map/cond/branch_1_fun/forward_first/pallas_call | solution.py:157
  9.6 2.5 %collective-permute-start.15 = (f32[2,512]{1,0:T(2,128)S(1)}, f32[2,512]{1,0:T(2,128)S(1)}, u32[]{:S(2)}, u32[]{:S(2)}) collective-permute-start(f32[2,512]{1,0:T(2,128)S(1)} %get-tuple-element.48.parts_0_), channel_id=1, source_target_pairs={{0,3},{1,2},{2,1},{3,0},{4,7},{5,6},{6,5},{7,4},{8,11},{9,10},{10,... | collective-permute-start | bytes 12296 | tf_op jit(solution)/shard_map/cond/branch_1_fun/ppermute | solution.py:456
  13.5 2.3 %collective-permute-done.14.parts_2_ = f32[2,512]{1,0:T(2,128)S(1)} collective-permute-done((f32[2,512]{1,0:T(2,128)S(1)}, f32[2,512]{1,0:T(2,128)S(1)}, u32[]{:S(2)}, u32[]{:S(2)}) %collective-permute-start.14) | collective-permute-done | bytes 4128 | tf_op jit(solution)/shard_map/cond/branch_1_fun/ppermute | solution.py:456
  15.8 10.6 %middle.4 = (bf16[2048,1792]{1,0:T(8,128)(2,1)S(1)}, f32[512,1792]{1,0:T(8,128)S(1)}, bf16[2048,512]{1,0:T(8,128)(2,1)S(1)}, f32[2,512]{1,0:T(2,128)S(1)}, f32[1,128]{1,0:T(1,128)S(1)}) custom-call(f32[2,512]{1,0:T(2,128)S(1)} %get-tuple-element.48.parts_0_, f32[2,512]{1,0:T(2,128)S(1)} %collective-permute-done.13.parts_1_, ...), custom_call_target="tpu_custom_call" | custom-call | tf_op jit(solution)/shard_map/cond/branch_1_fun/middle/pallas_call | solution.py:251
  26.4 1.2 collective-permute-start.17
  28.3 1.2 collective-permute-done.18.refs_3_
  30.1 1.2 branch_1_fun.7
  31.3 6.5 %branch_1_fun.12.own_ref = bf16[2048,512]{1,0:T(8,128)(2,1)S(1)} custom-call(f32[512,128]{1,0:T(8,128)S(1)} %get-tuple-element.60.by_target, f32[512,128]{1,0:T(8,128)S(1)} %get-tuple-element.61.by_hidden, bf16[2048,512]{1,0:T(8,128)(2,1)S(1)} %get-tuple-element.56.refs_4_.xt_ref, bf16[2048,1792]{1,0:T(8,128)(2,1)S(1)} %get-tuple-element.51.w_ref.refs_5_, ...), custom_call_target="tpu_custom_call" | custom-call | flops 1073741824 | bytes 9961472 | tf_op jit(solution)/shard_map/cond/branch_1_fun/pallas_call | solution.py:340
  37.7 6.5 %branch_1_fun.11.own_ref = bf16[2048,512]{1,0:T(8,128)(2,1)S(1)} custom-call(f32[512,128]{1,0:T(8,128)S(1)} %get-tuple-element.60.by_target, f32[512,128]{1,0:T(8,128)S(1)} %get-tuple-element.61.by_hidden, bf16[2048,512]{1,0:T(8,128)(2,1)S(1)} %get-tuple-element.56.refs_4_.xt_ref, bf16[2048,1792]{1,0:T(8,128)(2,1)S(1)} %get-tuple-element.51.w_ref.refs_5_, ...), custom_call_target="tpu_custom_call" | custom-call | flops 1073741824 | bytes 9961472 | tf_op jit(solution)/shard_map/cond/branch_1_fun/pallas_call | solution.py:340
  44.2 1.6 collective-permute-start.22
  45.8 1.6 collective-permute-start.23
  47.4 6.5 %branch_1_fun.10.own_ref = bf16[2048,512]{1,0:T(8,128)(2,1)S(1)} custom-call(f32[512,128]{1,0:T(8,128)S(1)} %get-tuple-element.60.by_target, f32[512,128]{1,0:T(8,128)S(1)} %get-tuple-element.61.by_hidden, bf16[2048,512]{1,0:T(8,128)(2,1)S(1)} %get-tuple-element.56.refs_4_.xt_ref, bf16[2048,1792]{1,0:T(8,128)(2,1)S(1)} %get-tuple-element.51.w_ref.refs_5_, ...), custom_call_target="tpu_custom_call" | custom-call | flops 1073741824 | bytes 9961472 | tf_op jit(solution)/shard_map/cond/branch_1_fun/pallas_call | solution.py:340
  53.9 1.6 collective-permute-start.21
  55.5 0.8 branch_1_fun.13.own_ref
  56.6 1.6 collective-permute-start.25
  58.2 0.8 branch_1_fun.9.own_ref
  59.0 0.8 branch_1_fun.8.own_ref
  59.9 130.2 %collective-permute-done.24.peer_ref = bf16[1024,128]{1,0:T(8,128)(2,1)S(1)} collective-permute-done((bf16[1024,128]{1,0:T(8,128)(2,1)S(1)}, bf16[1024,128]{1,0:T(8,128)(2,1)S(1)}, u32[]{:S(2)}, u32[]{:S(2)}) %collective-permute-start.24) | collective-permute-done | bytes 262176 | tf_op jit(solution)/shard_map/cond/branch_1_fun/ppermute | solution.py:463
  190.1 5.6 %collective-permute-done.25.peer_ref = bf16[1024,128]{1,0:T(8,128)(2,1)S(1)} collective-permute-done((bf16[1024,128]{1,0:T(8,128)(2,1)S(1)}, bf16[1024,128]{1,0:T(8,128)(2,1)S(1)}, u32[]{:S(2)}, u32[]{:S(2)}) %collective-permute-start.25) | collective-permute-done | bytes 262176 | tf_op jit(solution)/shard_map/cond/branch_1_fun/ppermute | solution.py:463
  197.8 1.7 mean.30.refs_0_
  199.5 1.7 mean.31.refs_0_
  201.2 1.7 mean.32.refs_0_
  203.7 1.9 collective-permute-done.19.peer_ref
  (20 shorter events, 6.7 us)
Async XLA Ops:
  9.6 3.8 %collective-permute-start.15 = (f32[2,512]{1,0:T(2,128)S(1)}, f32[2,512]{1,0:T(2,128)S(1)}, u32[]{:S(2)}, u32[]{:S(2)}) collective-permute-start(f32[2,512]{1,0:T(2,128)S(1)} %get-tuple-element.48.parts_0_), channel_id=1, source_target_pairs={{0,3},{1,2},{2,1},{3,0},{4,7},{5,6},{6,5},{7,4},{8,11},{9,10},{10,... | collective-permute-start | bytes 12296 | tf_op jit(solution)/shard_map/cond/branch_1_fun/ppermute | solution.py:456
  12.1 3.6 %collective-permute-start.14 = (f32[2,512]{1,0:T(2,128)S(1)}, f32[2,512]{1,0:T(2,128)S(1)}, u32[]{:S(2)}, u32[]{:S(2)}) collective-permute-start(f32[2,512]{1,0:T(2,128)S(1)} %get-tuple-element.48.parts_0_), channel_id=1, source_target_pairs={{0,2},{1,3},{2,0},{3,1},{4,6},{5,7},{6,4},{7,5},{8,10},{9,11},{10,... | collective-permute-start | bytes 12296 | tf_op jit(solution)/shard_map/cond/branch_1_fun/ppermute | solution.py:456
  12.8 3.0 %collective-permute-start.13 = (f32[2,512]{1,0:T(2,128)S(1)}, f32[2,512]{1,0:T(2,128)S(1)}, u32[]{:S(2)}, u32[]{:S(2)}) collective-permute-start(f32[2,512]{1,0:T(2,128)S(1)} %get-tuple-element.48.parts_0_), channel_id=1, source_target_pairs={{0,1},{1,0},{2,3},{3,2},{4,5},{5,4},{6,7},{7,6},{8,9},{9,8},{10,11... | collective-permute-start | bytes 12296 | tf_op jit(solution)/shard_map/cond/branch_1_fun/ppermute | solution.py:456
  26.3 3.1 %collective-permute-start.18 = (f32[2,512]{1,0:T(2,128)S(1)}, f32[2,512]{1,0:T(2,128)S(1)}, u32[]{:S(2)}, u32[]{:S(2)}) collective-permute-start(f32[2,512]{1,0:T(2,128)S(1)} %get-tuple-element.55.refs_0_), channel_id=1, source_target_pairs={{0,3},{1,2},{2,1},{3,0},{4,7},{5,6},{6,5},{7,4},{8,11},{9,10},{10,... | collective-permute-start | bytes 12296 | tf_op jit(solution)/shard_map/cond/branch_1_fun/ppermute | solution.py:456
  26.4 3.7 %collective-permute-start.17 = (f32[2,512]{1,0:T(2,128)S(1)}, f32[2,512]{1,0:T(2,128)S(1)}, u32[]{:S(2)}, u32[]{:S(2)}) collective-permute-start(f32[2,512]{1,0:T(2,128)S(1)} %get-tuple-element.55.refs_0_), channel_id=1, source_target_pairs={{0,2},{1,3},{2,0},{3,1},{4,6},{5,7},{6,4},{7,5},{8,10},{9,11},{10,... | collective-permute-start | bytes 12296 | tf_op jit(solution)/shard_map/cond/branch_1_fun/ppermute | solution.py:456
  27.6 2.5 %collective-permute-start.16 = (f32[2,512]{1,0:T(2,128)S(1)}, f32[2,512]{1,0:T(2,128)S(1)}, u32[]{:S(2)}, u32[]{:S(2)}) collective-permute-start(f32[2,512]{1,0:T(2,128)S(1)} %get-tuple-element.55.refs_0_), channel_id=1, source_target_pairs={{0,1},{1,0},{2,3},{3,2},{4,5},{5,4},{6,7},{7,6},{8,9},{9,8},{10,11... | collective-permute-start | bytes 12296 | tf_op jit(solution)/shard_map/cond/branch_1_fun/ppermute | solution.py:456
  44.2 155.3 %collective-permute-start.22 = (bf16[2048,512]{1,0:T(8,128)(2,1)S(1)}, bf16[2048,512]{1,0:T(8,128)(2,1)S(1)}, u32[]{:S(2)}, u32[]{:S(2)}) collective-permute-start(bf16[2048,512]{1,0:T(8,128)(2,1)S(1)} %branch_1_fun.11.own_ref), channel_id=1, source_target_pairs={{0,8},{4,12},{8,16},{12,20},{16,24},{20,28},{24,0},{28,4},{1,9},{5... | collective-permute-start | bytes 6291464 | tf_op jit(solution)/shard_map/cond/branch_1_fun/ppermute | solution.py:463
  45.8 152.0 %collective-permute-start.23 = (bf16[2048,512]{1,0:T(8,128)(2,1)S(1)}, bf16[2048,512]{1,0:T(8,128)(2,1)S(1)}, u32[]{:S(2)}, u32[]{:S(2)}) collective-permute-start(bf16[2048,512]{1,0:T(8,128)(2,1)S(1)} %branch_1_fun.12.own_ref), channel_id=1, source_target_pairs={{0,8},{4,12},{8,16},{12,20},{16,24},{20,28},{24,0},{28,4},{1,9},{5... | collective-permute-start | bytes 6291464 | tf_op jit(solution)/shard_map/cond/branch_1_fun/ppermute | solution.py:463
  53.9 147.3 %collective-permute-start.21 = (bf16[2048,512]{1,0:T(8,128)(2,1)S(1)}, bf16[2048,512]{1,0:T(8,128)(2,1)S(1)}, u32[]{:S(2)}, u32[]{:S(2)}) collective-permute-start(bf16[2048,512]{1,0:T(8,128)(2,1)S(1)} %branch_1_fun.10.own_ref), channel_id=1, source_target_pairs={{0,8},{4,12},{8,16},{12,20},{16,24},{20,28},{24,0},{28,4},{1,9},{5... | collective-permute-start | bytes 6291464 | tf_op jit(solution)/shard_map/cond/branch_1_fun/ppermute | solution.py:463
  56.4 133.7 %collective-permute-start.24 = (bf16[1024,128]{1,0:T(8,128)(2,1)S(1)}, bf16[1024,128]{1,0:T(8,128)(2,1)S(1)}, u32[]{:S(2)}, u32[]{:S(2)}) collective-permute-start(bf16[1024,128]{1,0:T(8,128)(2,1)S(1)} %branch_1_fun.13.own_ref), channel_id=1, source_target_pairs={{0,8},{4,12},{8,16},{12,20},{16,24},{20,28},{24,0},{28,4},{1,9},{5... | collective-permute-start | bytes 786440 | tf_op jit(solution)/shard_map/cond/branch_1_fun/ppermute | solution.py:463
  56.6 139.1 %collective-permute-start.25 = (bf16[1024,128]{1,0:T(8,128)(2,1)S(1)}, bf16[1024,128]{1,0:T(8,128)(2,1)S(1)}, u32[]{:S(2)}, u32[]{:S(2)}) collective-permute-start(bf16[1024,128]{1,0:T(8,128)(2,1)S(1)} %get-tuple-element.62.own_ref), channel_id=1, source_target_pairs={{0,8},{4,12},{8,16},{12,20},{16,24},{20,28},{24,0},{28,4},{1,9},{5... | collective-permute-start | bytes 786440 | tf_op jit(solution)/shard_map/cond/branch_1_fun/ppermute | solution.py:463
  190.1 12.8 %collective-permute-start.20 = (bf16[1024,128]{1,0:T(8,128)(2,1)S(1)}, bf16[1024,128]{1,0:T(8,128)(2,1)S(1)}, u32[]{:S(2)}, u32[]{:S(2)}) collective-permute-start(bf16[1024,128]{1,0:T(8,128)(2,1)S(1)} %branch_1_fun.9.own_ref), channel_id=1, source_target_pairs={{0,8},{4,12},{8,16},{12,20},{16,24},{20,28},{24,0},{28,4},{1,9},{5... | collective-permute-start | bytes 786440 | tf_op jit(solution)/shard_map/cond/branch_1_fun/ppermute | solution.py:463
  195.7 9.9 %collective-permute-start.19 = (bf16[1024,128]{1,0:T(8,128)(2,1)S(1)}, bf16[1024,128]{1,0:T(8,128)(2,1)S(1)}, u32[]{:S(2)}, u32[]{:S(2)}) collective-permute-start(bf16[1024,128]{1,0:T(8,128)(2,1)S(1)} %branch_1_fun.8.own_ref), channel_id=1, source_target_pairs={{0,8},{4,12},{8,16},{12,20},{16,24},{20,28},{24,0},{28,4},{1,9},{5... | collective-permute-start | bytes 786440 | tf_op jit(solution)/shard_map/cond/branch_1_fun/ppermute | solution.py:463

commit v5 on v4

--- a/solution.py
+++ b/solution.py
@@ -22,7 +22,8 @@
 ROWS = 256
 LANES = 128
 TOKEN_ROWS = 64
-PIECE_CELLS = 256 * 256
+FIRST_CELLS = 256 * 256
+PIECE_CELLS = 128 * 256
 MEAN_CELLS = 128 * 256
 PIECE_COLUMNS = 512
 AHEAD = 3
@@ -333,13 +334,14 @@
     last_part(by_target, by_hidden, *operands, final_ref, grad_rows, scale=scale, **sizes)
 
 
-def piece_call(kernel, outs, operands, tall, cols, count, units):
+def piece_call(kernel, name, outs, operands, tall, cols, count, units):
     whole = pl.BlockSpec(memory_space=pltpu.VMEM)
     height, block = tall.stop - tall.start, cols.stop - cols.start
     width = operands[-4].shape[0]
+    cells = PIECE_CELLS if name == "next_piece" else FIRST_CELLS
     return pl.pallas_call(
         functools.partial(
-            kernel, scale=width**-0.5, tall=tall, cols=cols, rows=min(PIECE_CELLS // block, height), **units
+            kernel, scale=width**-0.5, tall=tall, cols=cols, rows=min(cells // block, height), **units
         ),
         out_shape=(pltpu.VMEM((height, block), BF16), *outs),
         in_specs=[whole] * len(operands),
@@ -362,12 +364,14 @@
         jax.ShapeDtypeStruct((1, LANES), F32),
     )
     extra = {"units": units, "parts": len(stats)}
-    return piece_call(first_piece_kernel, outs, (*stats, *operands), tall, cols, count, extra)
+    return piece_call(
+        first_piece_kernel, "first_piece", outs, (*stats, *operands), tall, cols, count, extra
+    )
 
 
 def next_piece(factors, operands, tall, cols):
     count = operands[0].shape[1]
-    return piece_call(last_part, (), (*factors, *operands), tall, cols, count, {})[0]
+    return piece_call(last_part, "next_piece", (), (*factors, *operands), tall, cols, count, {})[0]
 
 
 def losses_kernel(first_ref, second_ref, out_ref, buffer, sem):

time: 207 us -> 212 us (1.024)
  Pallas kernels: 50.4 us -> 59 us
  waiting for transfers between devices: 142 us -> 139 us
    pallas_call x7, Pallas kernels: 23 us -> 31.6 us  [piece_call(): pl.pallas_call(functools.partial(kernel, scale=width ** (-0.5), tall=tall...]
    ppermute x7, waiting for transfers between devices: 138 us -> 134 us  [shifted(): lax.ppermute(array, axis, [(i, (i + by) % devices) for i in range(devices)])]
  transfers between devices with their start and end apart: 13 -> 13, of which waited for: 7 -> 7; matrix products, arithmetic and copies ran while one was open for 0% -> 0% of each run, Pallas kernels for 8% -> 10%
where the time goes in v5:
time: 212 us
  waiting for transfers between devices  139 us (66%)
  Pallas kernels  59 us (28%)
  starting transfers between devices  11.8 us (6%)
    ppermute x7, waiting for transfers between devices, shifted(): lax.ppermute(array, axis, [(i, (i + by) % devices) for i in range(devices)])  134 us
    pallas_call x7, Pallas kernels, piece_call(): pl.pallas_call(functools.partial(kernel, scale=width ** (-0.5), tall=tall...  31.6 us
    pallas_call x1, Pallas kernels, middle(): pl.pallas_call(functools.partial(middle_kernel, scale=width ** (-0.5), un...  10.6 us
    pallas_call x1, Pallas kernels, forward(): pl.pallas_call(functools.partial(forward_kernel, block=block), out_shape=...  8.15 us
    pallas_call x7, Pallas kernels, mean_into(): pl.pallas_call(functools.partial(mean_kernel, tall=tall, cols=cols, parts...  8.07 us
    ppermute x7, starting transfers between devices, shifted(): lax.ppermute(array, axis, [(i, (i + by) % devices) for i in range(devices)])  6.7 us
    ppermute x6, starting transfers between devices, everyones(): lax.ppermute(array, axis, [(i, i ^ flip) for i in range(devices)])  5.1 us
    ppermute x6, waiting for transfers between devices, everyones(): lax.ppermute(array, axis, [(i, i ^ flip) for i in range(devices)])  4.76 us
  transfers between devices with their start and end apart: 13, of which 7 were waited for; matrix products, arithmetic and copies ran while one was open for 0% of the time, Pallas kernels for 10%

profile of v5, /device:TPU:0, one launch (start us, length us, event | category | flops | bytes accessed | tf_op | source)
XLA Modules:
  0.0 212.2 jit_solution(1892333314176319661)
XLA Ops:
  1.3 210.7 %conditional.1 = (f32[1,2]{1,0:T(1,128)}, bf16[1,2048,1792]{2,1,0:T(8,128)(2,1)}) conditional(s32[]{:T(128)} %bitcast.3, (s32[2]{0:T(128)}, bf16[2,512,2048]{2,1,0:T(8,128)(2,1)}, bf16[2048,1792]{1,0:T(8,128)(2,1)}, bf16[2,512,1792]{2,1,0:T(8,128)(2,1)}) %tuple.37, (s32[2]{0:T(128)}, bf16[2,512,2048]{2,1,0:T(8,128)(2,1)}, ...), branch_computations={%region_0.0_spmd, %region_1.0_spmd, %region_2.0_spmd} | conditional | flops 3765436416 | bytes 90276376 | solution.py:503
  1.5 8.1 %forward_first.4 = (f32[512,1792]{1,0:T(8,128)S(1)}, bf16[2048,512]{1,0:T(8,128)(2,1)S(1)}, f32[2,512]{1,0:T(2,128)S(1)}, bf16[2,512,2048]{2,1,0:T(8,128)(2,1)S(...) custom-call(s32[2]{0:T(128)} %get-tuple-element.44.order_hbm, ...), custom_call_target="tpu_custom_call" | custom-call | tf_op jit(solution)/shard_map/cond/branch_1_fun/forward_first/pallas_call | solution.py:158
  9.6 2.5 %collective-permute-start.15 = (f32[2,512]{1,0:T(2,128)S(1)}, f32[2,512]{1,0:T(2,128)S(1)}, u32[]{:S(2)}, u32[]{:S(2)}) collective-permute-start(f32[2,512]{1,0:T(2,128)S(1)} %get-tuple-element.48.parts_0_), channel_id=1, source_target_pairs={{0,3},{1,2},{2,1},{3,0},{4,7},{5,6},{6,5},{7,4},{8,11},{9,10},{10,... | collective-permute-start | bytes 12296 | tf_op jit(solution)/shard_map/cond/branch_1_fun/ppermute | solution.py:460
  13.5 2.3 %collective-permute-done.14.parts_2_ = f32[2,512]{1,0:T(2,128)S(1)} collective-permute-done((f32[2,512]{1,0:T(2,128)S(1)}, f32[2,512]{1,0:T(2,128)S(1)}, u32[]{:S(2)}, u32[]{:S(2)}) %collective-permute-start.14) | collective-permute-done | bytes 4128 | tf_op jit(solution)/shard_map/cond/branch_1_fun/ppermute | solution.py:460
  15.8 10.6 %middle.4 = (bf16[2048,1792]{1,0:T(8,128)(2,1)S(1)}, f32[512,1792]{1,0:T(8,128)S(1)}, bf16[2048,512]{1,0:T(8,128)(2,1)S(1)}, f32[2,512]{1,0:T(2,128)S(1)}, f32[1,128]{1,0:T(1,128)S(1)}) custom-call(f32[2,512]{1,0:T(2,128)S(1)} %get-tuple-element.48.parts_0_, f32[2,512]{1,0:T(2,128)S(1)} %collective-permute-done.13.parts_1_, ...), custom_call_target="tpu_custom_call" | custom-call | tf_op jit(solution)/shard_map/cond/branch_1_fun/middle/pallas_call | solution.py:252
  26.4 1.2 collective-permute-start.17
  28.3 1.2 collective-permute-done.18.refs_3_
  30.1 1.2 branch_1_fun.7
  31.3 9.1 %branch_1_fun.12.own_ref = bf16[2048,512]{1,0:T(8,128)(2,1)S(1)} custom-call(f32[512,128]{1,0:T(8,128)S(1)} %get-tuple-element.60.by_target, f32[512,128]{1,0:T(8,128)S(1)} %get-tuple-element.61.by_hidden, bf16[2048,512]{1,0:T(8,128)(2,1)S(1)} %get-tuple-element.56.refs_4_.xt_ref, bf16[2048,1792]{1,0:T(8,128)(2,1)S(1)} %get-tuple-element.51.w_ref.refs_5_, ...), custom_call_target="tpu_custom_call" | custom-call | flops 1073741824 | bytes 9961472 | tf_op jit(solution)/shard_map/cond/branch_1_fun/pallas_call | solution.py:342
  40.4 9.0 %branch_1_fun.11.own_ref = bf16[2048,512]{1,0:T(8,128)(2,1)S(1)} custom-call(f32[512,128]{1,0:T(8,128)S(1)} %get-tuple-element.60.by_target, f32[512,128]{1,0:T(8,128)S(1)} %get-tuple-element.61.by_hidden, bf16[2048,512]{1,0:T(8,128)(2,1)S(1)} %get-tuple-element.56.refs_4_.xt_ref, bf16[2048,1792]{1,0:T(8,128)(2,1)S(1)} %get-tuple-element.51.w_ref.refs_5_, ...), custom_call_target="tpu_custom_call" | custom-call | flops 1073741824 | bytes 9961472 | tf_op jit(solution)/shard_map/cond/branch_1_fun/pallas_call | solution.py:342
  49.4 1.6 collective-permute-start.22
  51.0 1.6 collective-permute-start.23
  52.6 9.1 %branch_1_fun.10.own_ref = bf16[2048,512]{1,0:T(8,128)(2,1)S(1)} custom-call(f32[512,128]{1,0:T(8,128)S(1)} %get-tuple-element.60.by_target, f32[512,128]{1,0:T(8,128)S(1)} %get-tuple-element.61.by_hidden, bf16[2048,512]{1,0:T(8,128)(2,1)S(1)} %get-tuple-element.56.refs_4_.xt_ref, bf16[2048,1792]{1,0:T(8,128)(2,1)S(1)} %get-tuple-element.51.w_ref.refs_5_, ...), custom_call_target="tpu_custom_call" | custom-call | flops 1073741824 | bytes 9961472 | tf_op jit(solution)/shard_map/cond/branch_1_fun/pallas_call | solution.py:342
  61.7 1.6 collective-permute-start.21
  63.3 1.1 branch_1_fun.13.own_ref
  64.7 1.6 collective-permute-start.25
  66.3 1.1 branch_1_fun.9.own_ref
  67.4 1.1 branch_1_fun.8.own_ref
  68.5 126.8 %collective-permute-done.24.peer_ref = bf16[1024,128]{1,0:T(8,128)(2,1)S(1)} collective-permute-done((bf16[1024,128]{1,0:T(8,128)(2,1)S(1)}, bf16[1024,128]{1,0:T(8,128)(2,1)S(1)}, u32[]{:S(2)}, u32[]{:S(2)}) %collective-permute-start.24) | collective-permute-done | bytes 262176 | tf_op jit(solution)/shard_map/cond/branch_1_fun/ppermute | solution.py:467
  195.3 5.6 %collective-permute-done.25.peer_ref = bf16[1024,128]{1,0:T(8,128)(2,1)S(1)} collective-permute-done((bf16[1024,128]{1,0:T(8,128)(2,1)S(1)}, bf16[1024,128]{1,0:T(8,128)(2,1)S(1)}, u32[]{:S(2)}, u32[]{:S(2)}) %collective-permute-start.25) | collective-permute-done | bytes 262176 | tf_op jit(solution)/shard_map/cond/branch_1_fun/ppermute | solution.py:467
  203.0 1.7 mean.30.refs_0_
  204.7 1.7 mean.31.refs_0_
  206.4 1.7 mean.32.refs_0_
  208.9 1.8 collective-permute-done.19.peer_ref
  (20 shorter events, 6.7 us)
Async XLA Ops:
  9.6 3.8 %collective-permute-start.15 = (f32[2,512]{1,0:T(2,128)S(1)}, f32[2,512]{1,0:T(2,128)S(1)}, u32[]{:S(2)}, u32[]{:S(2)}) collective-permute-start(f32[2,512]{1,0:T(2,128)S(1)} %get-tuple-element.48.parts_0_), channel_id=1, source_target_pairs={{0,3},{1,2},{2,1},{3,0},{4,7},{5,6},{6,5},{7,4},{8,11},{9,10},{10,... | collective-permute-start | bytes 12296 | tf_op jit(solution)/shard_map/cond/branch_1_fun/ppermute | solution.py:460
  12.1 3.6 %collective-permute-start.14 = (f32[2,512]{1,0:T(2,128)S(1)}, f32[2,512]{1,0:T(2,128)S(1)}, u32[]{:S(2)}, u32[]{:S(2)}) collective-permute-start(f32[2,512]{1,0:T(2,128)S(1)} %get-tuple-element.48.parts_0_), channel_id=1, source_target_pairs={{0,2},{1,3},{2,0},{3,1},{4,6},{5,7},{6,4},{7,5},{8,10},{9,11},{10,... | collective-permute-start | bytes 12296 | tf_op jit(solution)/shard_map/cond/branch_1_fun/ppermute | solution.py:460
  12.8 3.0 %collective-permute-start.13 = (f32[2,512]{1,0:T(2,128)S(1)}, f32[2,512]{1,0:T(2,128)S(1)}, u32[]{:S(2)}, u32[]{:S(2)}) collective-permute-start(f32[2,512]{1,0:T(2,128)S(1)} %get-tuple-element.48.parts_0_), channel_id=1, source_target_pairs={{0,1},{1,0},{2,3},{3,2},{4,5},{5,4},{6,7},{7,6},{8,9},{9,8},{10,11... | collective-permute-start | bytes 12296 | tf_op jit(solution)/shard_map/cond/branch_1_fun/ppermute | solution.py:460
  26.3 3.1 %collective-permute-start.18 = (f32[2,512]{1,0:T(2,128)S(1)}, f32[2,512]{1,0:T(2,128)S(1)}, u32[]{:S(2)}, u32[]{:S(2)}) collective-permute-start(f32[2,512]{1,0:T(2,128)S(1)} %get-tuple-element.55.refs_0_), channel_id=1, source_target_pairs={{0,3},{1,2},{2,1},{3,0},{4,7},{5,6},{6,5},{7,4},{8,11},{9,10},{10,... | collective-permute-start | bytes 12296 | tf_op jit(solution)/shard_map/cond/branch_1_fun/ppermute | solution.py:460
  26.4 3.7 %collective-permute-start.17 = (f32[2,512]{1,0:T(2,128)S(1)}, f32[2,512]{1,0:T(2,128)S(1)}, u32[]{:S(2)}, u32[]{:S(2)}) collective-permute-start(f32[2,512]{1,0:T(2,128)S(1)} %get-tuple-element.55.refs_0_), channel_id=1, source_target_pairs={{0,2},{1,3},{2,0},{3,1},{4,6},{5,7},{6,4},{7,5},{8,10},{9,11},{10,... | collective-permute-start | bytes 12296 | tf_op jit(solution)/shard_map/cond/branch_1_fun/ppermute | solution.py:460
  27.6 2.5 %collective-permute-start.16 = (f32[2,512]{1,0:T(2,128)S(1)}, f32[2,512]{1,0:T(2,128)S(1)}, u32[]{:S(2)}, u32[]{:S(2)}) collective-permute-start(f32[2,512]{1,0:T(2,128)S(1)} %get-tuple-element.55.refs_0_), channel_id=1, source_target_pairs={{0,1},{1,0},{2,3},{3,2},{4,5},{5,4},{6,7},{7,6},{8,9},{9,8},{10,11... | collective-permute-start | bytes 12296 | tf_op jit(solution)/shard_map/cond/branch_1_fun/ppermute | solution.py:460
  49.4 155.3 %collective-permute-start.22 = (bf16[2048,512]{1,0:T(8,128)(2,1)S(1)}, bf16[2048,512]{1,0:T(8,128)(2,1)S(1)}, u32[]{:S(2)}, u32[]{:S(2)}) collective-permute-start(bf16[2048,512]{1,0:T(8,128)(2,1)S(1)} %branch_1_fun.11.own_ref), channel_id=1, source_target_pairs={{0,8},{4,12},{8,16},{12,20},{16,24},{20,28},{24,0},{28,4},{1,9},{5... | collective-permute-start | bytes 6291464 | tf_op jit(solution)/shard_map/cond/branch_1_fun/ppermute | solution.py:467
  51.0 152.0 %collective-permute-start.23 = (bf16[2048,512]{1,0:T(8,128)(2,1)S(1)}, bf16[2048,512]{1,0:T(8,128)(2,1)S(1)}, u32[]{:S(2)}, u32[]{:S(2)}) collective-permute-start(bf16[2048,512]{1,0:T(8,128)(2,1)S(1)} %branch_1_fun.12.own_ref), channel_id=1, source_target_pairs={{0,8},{4,12},{8,16},{12,20},{16,24},{20,28},{24,0},{28,4},{1,9},{5... | collective-permute-start | bytes 6291464 | tf_op jit(solution)/shard_map/cond/branch_1_fun/ppermute | solution.py:467
  61.7 144.7 %collective-permute-start.21 = (bf16[2048,512]{1,0:T(8,128)(2,1)S(1)}, bf16[2048,512]{1,0:T(8,128)(2,1)S(1)}, u32[]{:S(2)}, u32[]{:S(2)}) collective-permute-start(bf16[2048,512]{1,0:T(8,128)(2,1)S(1)} %branch_1_fun.10.own_ref), channel_id=1, source_target_pairs={{0,8},{4,12},{8,16},{12,20},{16,24},{20,28},{24,0},{28,4},{1,9},{5... | collective-permute-start | bytes 6291464 | tf_op jit(solution)/shard_map/cond/branch_1_fun/ppermute | solution.py:467
  64.4 130.8 %collective-permute-start.24 = (bf16[1024,128]{1,0:T(8,128)(2,1)S(1)}, bf16[1024,128]{1,0:T(8,128)(2,1)S(1)}, u32[]{:S(2)}, u32[]{:S(2)}) collective-permute-start(bf16[1024,128]{1,0:T(8,128)(2,1)S(1)} %branch_1_fun.13.own_ref), channel_id=1, source_target_pairs={{0,8},{4,12},{8,16},{12,20},{16,24},{20,28},{24,0},{28,4},{1,9},{5... | collective-permute-start | bytes 786440 | tf_op jit(solution)/shard_map/cond/branch_1_fun/ppermute | solution.py:467
  64.7 136.2 %collective-permute-start.25 = (bf16[1024,128]{1,0:T(8,128)(2,1)S(1)}, bf16[1024,128]{1,0:T(8,128)(2,1)S(1)}, u32[]{:S(2)}, u32[]{:S(2)}) collective-permute-start(bf16[1024,128]{1,0:T(8,128)(2,1)S(1)} %get-tuple-element.62.own_ref), channel_id=1, source_target_pairs={{0,8},{4,12},{8,16},{12,20},{16,24},{20,28},{24,0},{28,4},{1,9},{5... | collective-permute-start | bytes 786440 | tf_op jit(solution)/shard_map/cond/branch_1_fun/ppermute | solution.py:467
  195.3 12.8 %collective-permute-start.20 = (bf16[1024,128]{1,0:T(8,128)(2,1)S(1)}, bf16[1024,128]{1,0:T(8,128)(2,1)S(1)}, u32[]{:S(2)}, u32[]{:S(2)}) collective-permute-start(bf16[1024,128]{1,0:T(8,128)(2,1)S(1)} %branch_1_fun.9.own_ref), channel_id=1, source_target_pairs={{0,8},{4,12},{8,16},{12,20},{16,24},{20,28},{24,0},{28,4},{1,9},{5... | collective-permute-start | bytes 786440 | tf_op jit(solution)/shard_map/cond/branch_1_fun/ppermute | solution.py:467
  200.9 9.8 %collective-permute-start.19 = (bf16[1024,128]{1,0:T(8,128)(2,1)S(1)}, bf16[1024,128]{1,0:T(8,128)(2,1)S(1)}, u32[]{:S(2)}, u32[]{:S(2)}) collective-permute-start(bf16[1024,128]{1,0:T(8,128)(2,1)S(1)} %branch_1_fun.8.own_ref), channel_id=1, source_target_pairs={{0,8},{4,12},{8,16},{12,20},{16,24},{20,28},{24,0},{28,4},{1,9},{5... | collective-permute-start | bytes 786440 | tf_op jit(solution)/shard_map/cond/branch_1_fun/ppermute | solution.py:467

commit v6 on v4

--- a/solution.py
+++ b/solution.py
@@ -22,9 +22,7 @@
 ROWS = 256
 LANES = 128
 TOKEN_ROWS = 64
-PIECE_CELLS = 256 * 256
-MEAN_CELLS = 128 * 256
-PIECE_COLUMNS = 512
+PIECE_COLUMNS = 384
 AHEAD = 3
 
 
@@ -339,7 +337,7 @@
     width = operands[-4].shape[0]
     return pl.pallas_call(
         functools.partial(
-            kernel, scale=width**-0.5, tall=tall, cols=cols, rows=min(PIECE_CELLS // block, height), **units
+            kernel, scale=width**-0.5, tall=tall, cols=cols, rows=min(512 if block <= LANES else 128, height), **units
         ),
         out_shape=(pltpu.VMEM((height, block), BF16), *outs),
         in_specs=[whole] * len(operands),
@@ -395,7 +393,7 @@
     out_ref, buffer, sems = refs[-3:]
     height, block = own_ref.shape
     rows = height // parts
-    step = min(MEAN_CELLS // block, rows)
+    step = min(256 if block <= LANES else 64, rows)
 
     def copy(at):
         part = pl.ds(pl.multiple_of(at * rows, rows), rows)

time: 207 us -> 205 us (level)
  waiting for transfers between devices: 142 us -> 137 us
  Pallas kernels: 50.4 us -> 53.7 us
    ppermute x7 -> x8, waiting for transfers between devices: 138 us -> 132 us  [shifted(): lax.ppermute(array, axis, [(i, (i + by) % devices) for i in range(devices)])]
    pallas_call x7 -> x8, Pallas kernels: 23 us -> 25.4 us  [piece_call(): pl.pallas_call(functools.partial(kernel, scale=width ** (-0.5), tall=tall...]
    pallas_call x7 -> x8, Pallas kernels: 8.07 us -> 9.08 us  [mean_into(): pl.pallas_call(functools.partial(mean_kernel, tall=tall, cols=cols, parts...]
    ppermute x7 -> x8, starting transfers between devices: 6.7 us -> 6.8 us  [shifted(): lax.ppermute(array, axis, [(i, (i + by) % devices) for i in range(devices)])]
  transfers between devices with their start and end apart: 13 -> 14, of which waited for: 7 -> 8; matrix products, arithmetic and copies ran while one was open for 0% -> 0% of each run, Pallas kernels for 8% -> 14%
where the time goes in v6:
time: 205 us
  waiting for transfers between devices  137 us (67%)
  Pallas kernels  53.7 us (26%)
  starting transfers between devices  11.9 us (6%)
    ppermute x8, waiting for transfers between devices, shifted(): lax.ppermute(array, axis, [(i, (i + by) % devices) for i in range(devices)])  132 us
    pallas_call x8, Pallas kernels, piece_call(): pl.pallas_call(functools.partial(kernel, scale=width ** (-0.5), tall=tall...  25.4 us
    pallas_call x1, Pallas kernels, middle(): pl.pallas_call(functools.partial(middle_kernel, scale=width ** (-0.5), un...  10.6 us
    pallas_call x8, Pallas kernels, mean_into(): pl.pallas_call(functools.partial(mean_kernel, tall=tall, cols=cols, parts...  9.08 us
    pallas_call x1, Pallas kernels, forward(): pl.pallas_call(functools.partial(forward_kernel, block=block), out_shape=...  8.15 us
    ppermute x8, starting transfers between devices, shifted(): lax.ppermute(array, axis, [(i, (i + by) % devices) for i in range(devices)])  6.8 us
    ppermute x6, starting transfers between devices, everyones(): lax.ppermute(array, axis, [(i, i ^ flip) for i in range(devices)])  5.1 us
    ppermute x6, waiting for transfers between devices, everyones(): lax.ppermute(array, axis, [(i, i ^ flip) for i in range(devices)])  4.76 us
  transfers between devices with their start and end apart: 14, of which 8 were waited for; matrix products, arithmetic and copies ran while one was open for 0% of the time, Pallas kernels for 14%

profile of v6, /device:TPU:0, one launch (start us, length us, event | category | flops | bytes accessed | tf_op | source)
XLA Modules:
  0.0 204.8 jit_solution(10103468511179575508)
XLA Ops:
  1.3 203.4 %conditional.1 = (f32[1,2]{1,0:T(1,128)}, bf16[1,2048,1792]{2,1,0:T(8,128)(2,1)}) conditional(s32[]{:T(128)} %bitcast.3, (s32[2]{0:T(128)}, bf16[2,512,2048]{2,1,0:T(8,128)(2,1)}, bf16[2048,1792]{1,0:T(8,128)(2,1)}, bf16[2,512,1792]{2,1,0:T(8,128)(2,1)}) %tuple.37, (s32[2]{0:T(128)}, bf16[2,512,2048]{2,1,0:T(8,128)(2,1)}, ...), branch_computations={%region_0.0_spmd, %region_1.0_spmd, %region_2.0_spmd} | conditional | flops 3765436416 | bytes 92373568 | solution.py:497
  1.5 8.1 %forward_first.4 = (f32[512,1792]{1,0:T(8,128)S(1)}, bf16[2048,512]{1,0:T(8,128)(2,1)S(1)}, f32[2,512]{1,0:T(2,128)S(1)}, bf16[2,512,2048]{2,1,0:T(8,128)(2,1)S(...) custom-call(s32[2]{0:T(128)} %get-tuple-element.44.order_hbm, ...), custom_call_target="tpu_custom_call" | custom-call | tf_op jit(solution)/shard_map/cond/branch_1_fun/forward_first/pallas_call | solution.py:155
  9.6 2.5 %collective-permute-start.16 = (f32[2,512]{1,0:T(2,128)S(1)}, f32[2,512]{1,0:T(2,128)S(1)}, u32[]{:S(2)}, u32[]{:S(2)}) collective-permute-start(f32[2,512]{1,0:T(2,128)S(1)} %get-tuple-element.48.parts_0_), channel_id=1, source_target_pairs={{0,3},{1,2},{2,1},{3,0},{4,7},{5,6},{6,5},{7,4},{8,11},{9,10},{10,... | collective-permute-start | bytes 12296 | tf_op jit(solution)/shard_map/cond/branch_1_fun/ppermute | solution.py:454
  13.5 2.3 %collective-permute-done.15.parts_2_ = f32[2,512]{1,0:T(2,128)S(1)} collective-permute-done((f32[2,512]{1,0:T(2,128)S(1)}, f32[2,512]{1,0:T(2,128)S(1)}, u32[]{:S(2)}, u32[]{:S(2)}) %collective-permute-start.15) | collective-permute-done | bytes 4128 | tf_op jit(solution)/shard_map/cond/branch_1_fun/ppermute | solution.py:454
  15.8 10.6 %middle.4 = (bf16[2048,1792]{1,0:T(8,128)(2,1)S(1)}, f32[512,1792]{1,0:T(8,128)S(1)}, bf16[2048,512]{1,0:T(8,128)(2,1)S(1)}, f32[2,512]{1,0:T(2,128)S(1)}, f32[1,128]{1,0:T(1,128)S(1)}) custom-call(f32[2,512]{1,0:T(2,128)S(1)} %get-tuple-element.48.parts_0_, f32[2,512]{1,0:T(2,128)S(1)} %collective-permute-done.14.parts_1_, ...), custom_call_target="tpu_custom_call" | custom-call | tf_op jit(solution)/shard_map/cond/branch_1_fun/middle/pallas_call | solution.py:249
  26.4 1.2 collective-permute-start.18
  28.3 1.2 collective-permute-done.19.refs_3_
  30.1 1.2 branch_1_fun.8
  31.3 5.4 %branch_1_fun.14.own_ref = bf16[2048,384]{1,0:T(8,128)(2,1)S(1)} custom-call(f32[512,128]{1,0:T(8,128)S(1)} %get-tuple-element.60.by_target, f32[512,128]{1,0:T(8,128)S(1)} %get-tuple-element.61.by_hidden, bf16[2048,512]{1,0:T(8,128)(2,1)S(1)} %get-tuple-element.56.refs_4_.xt_ref, bf16[2048,1792]{1,0:T(8,128)(2,1)S(1)} %get-tuple-element.51.w_ref.refs_5_, ...), custom_call_target="tpu_custom_call" | custom-call | flops 805306368 | bytes 7995392 | tf_op jit(solution)/shard_map/cond/branch_1_fun/pallas_call | solution.py:338
  36.7 1.6 collective-permute-start.25
  38.3 5.4 %branch_1_fun.12.own_ref = bf16[2048,384]{1,0:T(8,128)(2,1)S(1)} custom-call(f32[512,128]{1,0:T(8,128)S(1)} %get-tuple-element.60.by_target, f32[512,128]{1,0:T(8,128)S(1)} %get-tuple-element.61.by_hidden, bf16[2048,512]{1,0:T(8,128)(2,1)S(1)} %get-tuple-element.56.refs_4_.xt_ref, bf16[2048,1792]{1,0:T(8,128)(2,1)S(1)} %get-tuple-element.51.w_ref.refs_5_, ...), custom_call_target="tpu_custom_call" | custom-call | flops 805306368 | bytes 7995392 | tf_op jit(solution)/shard_map/cond/branch_1_fun/pallas_call | solution.py:338
  43.8 1.6 collective-permute-start.23
  45.4 5.4 %branch_1_fun.13.own_ref = bf16[2048,384]{1,0:T(8,128)(2,1)S(1)} custom-call(f32[512,128]{1,0:T(8,128)S(1)} %get-tuple-element.60.by_target, f32[512,128]{1,0:T(8,128)S(1)} %get-tuple-element.61.by_hidden, bf16[2048,512]{1,0:T(8,128)(2,1)S(1)} %get-tuple-element.56.refs_4_.xt_ref, bf16[2048,1792]{1,0:T(8,128)(2,1)S(1)} %get-tuple-element.51.w_ref.refs_5_, ...), custom_call_target="tpu_custom_call" | custom-call | flops 805306368 | bytes 7995392 | tf_op jit(solution)/shard_map/cond/branch_1_fun/pallas_call | solution.py:338
  50.8 1.6 collective-permute-start.24
  52.5 5.4 %branch_1_fun.11.own_ref = bf16[2048,384]{1,0:T(8,128)(2,1)S(1)} custom-call(f32[512,128]{1,0:T(8,128)S(1)} %get-tuple-element.60.by_target, f32[512,128]{1,0:T(8,128)S(1)} %get-tuple-element.61.by_hidden, bf16[2048,512]{1,0:T(8,128)(2,1)S(1)} %get-tuple-element.56.refs_4_.xt_ref, bf16[2048,1792]{1,0:T(8,128)(2,1)S(1)} %get-tuple-element.51.w_ref.refs_5_, ...), custom_call_target="tpu_custom_call" | custom-call | flops 805306368 | bytes 7995392 | tf_op jit(solution)/shard_map/cond/branch_1_fun/pallas_call | solution.py:338
  59.0 1.6 collective-permute-start.26
  60.6 120.5 %collective-permute-done.26.peer_ref = bf16[1024,128]{1,0:T(8,128)(2,1)S(1)} collective-permute-done((bf16[1024,128]{1,0:T(8,128)(2,1)S(1)}, bf16[1024,128]{1,0:T(8,128)(2,1)S(1)}, u32[]{:S(2)}, u32[]{:S(2)}) %collective-permute-start.26) | collective-permute-done | bytes 262176 | tf_op jit(solution)/shard_map/cond/branch_1_fun/ppermute | solution.py:461
  182.9 7.1 %collective-permute-done.27.peer_ref = bf16[1024,128]{1,0:T(8,128)(2,1)S(1)} collective-permute-done((bf16[1024,128]{1,0:T(8,128)(2,1)S(1)}, bf16[1024,128]{1,0:T(8,128)(2,1)S(1)}, u32[]{:S(2)}, u32[]{:S(2)}) %collective-permute-start.27) | collective-permute-done | bytes 262176 | tf_op jit(solution)/shard_map/cond/branch_1_fun/ppermute | solution.py:461
  192.1 1.5 mean.34.refs_0_
  193.6 1.5 mean.35.refs_0_
  195.1 1.5 mean.36.refs_0_
  196.6 1.5 mean.37.refs_0_
  198.2 2.4 %collective-permute-done.21.peer_ref = bf16[1024,128]{1,0:T(8,128)(2,1)S(1)} collective-permute-done((bf16[1024,128]{1,0:T(8,128)(2,1)S(1)}, bf16[1024,128]{1,0:T(8,128)(2,1)S(1)}, u32[]{:S(2)}, u32[]{:S(2)}) %collective-permute-start.21) | collective-permute-done | bytes 262176 | tf_op jit(solution)/shard_map/cond/branch_1_fun/ppermute | solution.py:461
  201.4 2.0 collective-permute-done.20.peer_ref
  (24 shorter events, 9.1 us)
Async XLA Ops:
  9.6 3.8 %collective-permute-start.16 = (f32[2,512]{1,0:T(2,128)S(1)}, f32[2,512]{1,0:T(2,128)S(1)}, u32[]{:S(2)}, u32[]{:S(2)}) collective-permute-start(f32[2,512]{1,0:T(2,128)S(1)} %get-tuple-element.48.parts_0_), channel_id=1, source_target_pairs={{0,3},{1,2},{2,1},{3,0},{4,7},{5,6},{6,5},{7,4},{8,11},{9,10},{10,... | collective-permute-start | bytes 12296 | tf_op jit(solution)/shard_map/cond/branch_1_fun/ppermute | solution.py:454
  12.1 3.6 %collective-permute-start.15 = (f32[2,512]{1,0:T(2,128)S(1)}, f32[2,512]{1,0:T(2,128)S(1)}, u32[]{:S(2)}, u32[]{:S(2)}) collective-permute-start(f32[2,512]{1,0:T(2,128)S(1)} %get-tuple-element.48.parts_0_), channel_id=1, source_target_pairs={{0,2},{1,3},{2,0},{3,1},{4,6},{5,7},{6,4},{7,5},{8,10},{9,11},{10,... | collective-permute-start | bytes 12296 | tf_op jit(solution)/shard_map/cond/branch_1_fun/ppermute | solution.py:454
  12.8 3.0 %collective-permute-start.14 = (f32[2,512]{1,0:T(2,128)S(1)}, f32[2,512]{1,0:T(2,128)S(1)}, u32[]{:S(2)}, u32[]{:S(2)}) collective-permute-start(f32[2,512]{1,0:T(2,128)S(1)} %get-tuple-element.48.parts_0_), channel_id=1, source_target_pairs={{0,1},{1,0},{2,3},{3,2},{4,5},{5,4},{6,7},{7,6},{8,9},{9,8},{10,11... | collective-permute-start | bytes 12296 | tf_op jit(solution)/shard_map/cond/branch_1_fun/ppermute | solution.py:454
  26.3 3.1 %collective-permute-start.19 = (f32[2,512]{1,0:T(2,128)S(1)}, f32[2,512]{1,0:T(2,128)S(1)}, u32[]{:S(2)}, u32[]{:S(2)}) collective-permute-start(f32[2,512]{1,0:T(2,128)S(1)} %get-tuple-element.55.refs_0_), channel_id=1, source_target_pairs={{0,3},{1,2},{2,1},{3,0},{4,7},{5,6},{6,5},{7,4},{8,11},{9,10},{10,... | collective-permute-start | bytes 12296 | tf_op jit(solution)/shard_map/cond/branch_1_fun/ppermute | solution.py:454
  26.4 3.7 %collective-permute-start.18 = (f32[2,512]{1,0:T(2,128)S(1)}, f32[2,512]{1,0:T(2,128)S(1)}, u32[]{:S(2)}, u32[]{:S(2)}) collective-permute-start(f32[2,512]{1,0:T(2,128)S(1)} %get-tuple-element.55.refs_0_), channel_id=1, source_target_pairs={{0,2},{1,3},{2,0},{3,1},{4,6},{5,7},{6,4},{7,5},{8,10},{9,11},{10,... | collective-permute-start | bytes 12296 | tf_op jit(solution)/shard_map/cond/branch_1_fun/ppermute | solution.py:454
  27.6 2.5 %collective-permute-start.17 = (f32[2,512]{1,0:T(2,128)S(1)}, f32[2,512]{1,0:T(2,128)S(1)}, u32[]{:S(2)}, u32[]{:S(2)}) collective-permute-start(f32[2,512]{1,0:T(2,128)S(1)} %get-tuple-element.55.refs_0_), channel_id=1, source_target_pairs={{0,1},{1,0},{2,3},{3,2},{4,5},{5,4},{6,7},{7,6},{8,9},{9,8},{10,11... | collective-permute-start | bytes 12296 | tf_op jit(solution)/shard_map/cond/branch_1_fun/ppermute | solution.py:454
  36.7 153.2 %collective-permute-start.25 = (bf16[2048,384]{1,0:T(8,128)(2,1)S(1)}, bf16[2048,384]{1,0:T(8,128)(2,1)S(1)}, u32[]{:S(2)}, u32[]{:S(2)}) collective-permute-start(bf16[2048,384]{1,0:T(8,128)(2,1)S(1)} %branch_1_fun.14.own_ref), channel_id=1, source_target_pairs={{0,8},{4,12},{8,16},{12,20},{16,24},{20,28},{24,0},{28,4},{1,9},{5... | collective-permute-start | bytes 4718600 | tf_op jit(solution)/shard_map/cond/branch_1_fun/ppermute | solution.py:461
  43.8 151.3 %collective-permute-start.23 = (bf16[2048,384]{1,0:T(8,128)(2,1)S(1)}, bf16[2048,384]{1,0:T(8,128)(2,1)S(1)}, u32[]{:S(2)}, u32[]{:S(2)}) collective-permute-start(bf16[2048,384]{1,0:T(8,128)(2,1)S(1)} %branch_1_fun.12.own_ref), channel_id=1, source_target_pairs={{0,8},{4,12},{8,16},{12,20},{16,24},{20,28},{24,0},{28,4},{1,9},{5... | collective-permute-start | bytes 4718600 | tf_op jit(solution)/shard_map/cond/branch_1_fun/ppermute | solution.py:461
  50.8 142.7 %collective-permute-start.24 = (bf16[2048,384]{1,0:T(8,128)(2,1)S(1)}, bf16[2048,384]{1,0:T(8,128)(2,1)S(1)}, u32[]{:S(2)}, u32[]{:S(2)}) collective-permute-start(bf16[2048,384]{1,0:T(8,128)(2,1)S(1)} %branch_1_fun.13.own_ref), channel_id=1, source_target_pairs={{0,8},{4,12},{8,16},{12,20},{16,24},{20,28},{24,0},{28,4},{1,9},{5... | collective-permute-start | bytes 4718600 | tf_op jit(solution)/shard_map/cond/branch_1_fun/ppermute | solution.py:461
  57.9 138.7 %collective-permute-start.22 = (bf16[2048,384]{1,0:T(8,128)(2,1)S(1)}, bf16[2048,384]{1,0:T(8,128)(2,1)S(1)}, u32[]{:S(2)}, u32[]{:S(2)}) collective-permute-start(bf16[2048,384]{1,0:T(8,128)(2,1)S(1)} %branch_1_fun.11.own_ref), channel_id=1, source_target_pairs={{0,8},{4,12},{8,16},{12,20},{16,24},{20,28},{24,0},{28,4},{1,9},{5... | collective-permute-start | bytes 4718600 | tf_op jit(solution)/shard_map/cond/branch_1_fun/ppermute | solution.py:461
  59.0 122.2 %collective-permute-start.26 = (bf16[1024,128]{1,0:T(8,128)(2,1)S(1)}, bf16[1024,128]{1,0:T(8,128)(2,1)S(1)}, u32[]{:S(2)}, u32[]{:S(2)}) collective-permute-start(bf16[1024,128]{1,0:T(8,128)(2,1)S(1)} %branch_1_fun.15.own_ref), channel_id=1, source_target_pairs={{0,8},{4,12},{8,16},{12,20},{16,24},{20,28},{24,0},{28,4},{1,9},{5... | collective-permute-start | bytes 786440 | tf_op jit(solution)/shard_map/cond/branch_1_fun/ppermute | solution.py:461
  181.2 8.7 %collective-permute-start.27 = (bf16[1024,128]{1,0:T(8,128)(2,1)S(1)}, bf16[1024,128]{1,0:T(8,128)(2,1)S(1)}, u32[]{:S(2)}, u32[]{:S(2)}) collective-permute-start(bf16[1024,128]{1,0:T(8,128)(2,1)S(1)} %get-tuple-element.62.own_ref), channel_id=1, source_target_pairs={{0,8},{4,12},{8,16},{12,20},{16,24},{20,28},{24,0},{28,4},{1,9},{5... | collective-permute-start | bytes 786440 | tf_op jit(solution)/shard_map/cond/branch_1_fun/ppermute | solution.py:461
  189.9 10.7 %collective-permute-start.21 = (bf16[1024,128]{1,0:T(8,128)(2,1)S(1)}, bf16[1024,128]{1,0:T(8,128)(2,1)S(1)}, u32[]{:S(2)}, u32[]{:S(2)}) collective-permute-start(bf16[1024,128]{1,0:T(8,128)(2,1)S(1)} %branch_1_fun.10.own_ref), channel_id=1, source_target_pairs={{0,8},{4,12},{8,16},{12,20},{16,24},{20,28},{24,0},{28,4},{1,9},{5... | collective-permute-start | bytes 786440 | tf_op jit(solution)/shard_map/cond/branch_1_fun/ppermute | solution.py:461
  189.9 13.5 %collective-permute-start.20 = (bf16[1024,128]{1,0:T(8,128)(2,1)S(1)}, bf16[1024,128]{1,0:T(8,128)(2,1)S(1)}, u32[]{:S(2)}, u32[]{:S(2)}) collective-permute-start(bf16[1024,128]{1,0:T(8,128)(2,1)S(1)} %branch_1_fun.9.own_ref), channel_id=1, source_target_pairs={{0,8},{4,12},{8,16},{12,20},{16,24},{20,28},{24,0},{28,4},{1,9},{5... | collective-permute-start | bytes 786440 | tf_op jit(solution)/shard_map/cond/branch_1_fun/ppermute | solution.py:461
